TPU v7x, 32 devices: a whole 2x2x4 slice. The times are simulated.
32 devices in a mesh: dp: 16 (over z, x, core), axial: 2 (over y).
Axes of the slice: x: 2, y: 2, z: 4, core: 2. Of those that a mesh axis runs over, the one named last changes fastest.
Arguments:
- homolog_activations: bfloat16 [16, 32, 16, 256], P('dp', None, 'axial'), may hold values from -6 to 6
- homolog_adjoint: bfloat16 [16, 32, 16, 256], P('dp', None, 'axial'), may hold values from -6 to 6
- duplex_adjoint: bfloat16 [16, 16, 16, 128], P('dp', 'axial'), may hold values from -6 to 6
- homolog_exists_filter: int32 [16, 32], P('dp'), may hold values 0 or 1
- amino_exists_filter: int32 [16, 16], P('dp'), may hold values 0 or 1
- focus_matrices_tier: bfloat16 [5, 256, 256], replicated, may hold values from -0.375 to 0.375
- affine_parameters: float32 [5, 256], replicated, may hold values from -1.5 to 1.75, as said below
- left_right_matrices: bfloat16 [256, 64], replicated, may hold values from -0.375 to 0.375
- outer_final_matrix: bfloat16 [1024, 128], replicated, may hold values from -0.1875 to 0.1875
Outputs:
- homolog_derivative: bfloat16 [16, 32, 16, 256], P('dp', None, 'axial')
- grad_attention: float32 [5, 256, 256], replicated
- grad_vectors: float32 [5, 256], replicated
- grad_proj: float32 [256, 64], replicated
- pair_weight_gradient: float32 [1024, 128], replicated
Inputs may be any that keep to these rules, and one draw needn't show every extreme that they name: `affine_parameters`: gains near one, biases near zero.
All inputs are finite; a program needn't handle non-finite values. No bound on the sum of `homolog_exists_filter` or of `amino_exists_filter` on one device may be relied on, other than what follows from the above.
Results may differ from a plain program's by a relative error of at most 0.018.
Values may be sent and summed in bfloat16 or wider, within the bound.
No kernel may reach another device: no remote copies, remote signals or barrier semaphores. Data moves between devices by JAX's collectives and lax.ppermute only.
A program may use at most 64 MiB of HBM per device.

v0:
```python
from functools import partial

import jax
import jax.numpy as jnp
from jax import lax
from jax.sharding import PartitionSpec as P

HEADS = 8
HEAD_DIM = 32
OUTER_FACTORS = 32
DUPLEX_FEATURES = 128


def layer_normalize(values, scale_row, shift_row):
    average = jnp.mean(values, axis=-1, keepdims=True)
    centered = values - average
    spread = jnp.mean(centered * centered, axis=-1, keepdims=True)
    return centered * lax.rsqrt(spread + 1e-05) * scale_row + shift_row


def column_attention_block(
    sequence_flags,
    residue_flags,
    alignment_block,
    focus_matrices_tier,
    affine_parameters,
    left_right_matrices,
):
    sequence_total, present_row_count, channel_width = alignment_block.shape
    normalized_input = layer_normalize(
        alignment_block.astype(jnp.float32), affine_parameters[0], affine_parameters[1]
    ).astype(jnp.bfloat16)
    flat_rows = normalized_input.reshape(sequence_total * present_row_count, channel_width)
    shape_heads = (sequence_total, present_row_count, HEADS, HEAD_DIM)
    queries = (
        (
            jnp.dot(flat_rows, focus_matrices_tier[0], preferred_element_type=jnp.float32)
            * HEAD_DIM ** (-0.5)
        )
        .astype(jnp.bfloat16)
        .reshape(shape_heads)
    )
    keys_all = (
        jnp.dot(flat_rows, focus_matrices_tier[1], preferred_element_type=jnp.float32)
        .astype(jnp.bfloat16)
        .reshape(shape_heads)
    )
    values_all = (
        jnp.dot(flat_rows, focus_matrices_tier[2], preferred_element_type=jnp.float32)
        .astype(jnp.bfloat16)
        .reshape(shape_heads)
    )
    gate_value = jax.nn.sigmoid(
        jnp.dot(flat_rows, focus_matrices_tier[3], preferred_element_type=jnp.float32)
        + affine_parameters[2]
    )
    logits = jnp.einsum("srhd,trhd->rhst", queries, keys_all, preferred_element_type=jnp.float32)
    mask_bias = (sequence_flags.astype(jnp.float32) - 1.0) * 1000000000.0
    probs = jax.nn.softmax(logits + mask_bias[None, None, None, :], axis=-1).astype(jnp.bfloat16)
    attended = jnp.einsum("rhst,trhd->srhd", probs, values_all, preferred_element_type=jnp.float32)
    gated = (
        attended.reshape(sequence_total * present_row_count, channel_width) * gate_value
    ).astype(jnp.bfloat16)
    rows_update = jnp.dot(gated, focus_matrices_tier[4], preferred_element_type=jnp.float32)
    updated_alignment = alignment_block.astype(jnp.float32) + rows_update.reshape(
        sequence_total, present_row_count, channel_width
    )
    second = (
        layer_normalize(updated_alignment, affine_parameters[3], affine_parameters[4])
        .astype(jnp.bfloat16)
        .reshape(sequence_total * present_row_count, channel_width)
    )
    projected = jnp.dot(second, left_right_matrices, preferred_element_type=jnp.float32).reshape(
        sequence_total, present_row_count, 2 * OUTER_FACTORS
    )
    flags = (sequence_flags[:, None] * residue_flags[None, :]).astype(jnp.float32)
    projected = (projected * flags[:, :, None]).astype(jnp.bfloat16)
    return (updated_alignment, projected[:, :, :OUTER_FACTORS], projected[:, :, OUTER_FACTORS:])


def pair_block(left_part, right_part, outer_final_matrix, flags_rows, flags_cols, seq_total):
    outer = jnp.einsum("sic,sje->ijce", left_part, right_part, precision=lax.Precision.HIGHEST)
    rows_i, cols_j = (outer.shape[0], outer.shape[1])
    outer_flat = outer.reshape(rows_i * cols_j, OUTER_FACTORS * OUTER_FACTORS).astype(jnp.bfloat16)
    pair_rows = jnp.dot(outer_flat, outer_final_matrix, preferred_element_type=jnp.float32).reshape(
        rows_i, cols_j, DUPLEX_FEATURES
    )
    divisor = jnp.maximum(flags_rows[:, None] * flags_cols[None, :] * seq_total, 1.0)
    return pair_rows / divisor[:, :, None]


def per_device(
    homolog_activations,
    homolog_adjoint,
    duplex_adjoint,
    homolog_exists_filter,
    amino_exists_filter,
    focus_matrices_tier,
    affine_parameters,
    left_right_matrices,
    outer_final_matrix,
):
    shard_homologs = homolog_activations[0]
    local_cotangent = homolog_adjoint[0]
    pair_update_cotangent = duplex_adjoint[0]
    sequence_flags = homolog_exists_filter[0]
    residue_flags = amino_exists_filter[0]
    present_row_count = shard_homologs.shape[1]
    own_index = lax.axis_index("axial")
    own_flags = lax.dynamic_slice_in_dim(
        residue_flags, own_index * present_row_count, present_row_count
    )
    seq_total = jnp.sum(sequence_flags.astype(jnp.float32))
    res_float = residue_flags.astype(jnp.float32)
    own_float = own_flags.astype(jnp.float32)
    local_function = partial(column_attention_block, sequence_flags, own_flags)
    step_outputs, backward_function = jax.vjp(
        local_function, shard_homologs, focus_matrices_tier, affine_parameters, left_right_matrices
    )
    left_own, right_own = lax.optimization_barrier((step_outputs[1], step_outputs[2]))
    left_float = left_own.astype(jnp.float32)
    right_all = lax.all_gather(right_own, "axial", axis=1, tiled=True)

    def pair_fn(left_part, right_part, weight_part):
        return pair_block(left_part, right_part, weight_part, own_float, res_float, seq_total)

    unused, back_pair = jax.vjp(
        pair_fn, left_float, right_all.astype(jnp.float32), outer_final_matrix
    )
    left_cot, right_cot, pair_weight_cot = back_pair(pair_update_cotangent.astype(jnp.float32))
    right_grad = lax.psum_scatter(
        right_cot.astype(jnp.bfloat16), "axial", scatter_dimension=1, tiled=True
    )
    pair_weight_gradient = pair_weight_cot.astype(jnp.float32)
    cotangent_list = (
        local_cotangent.astype(jnp.float32),
        left_cot.astype(jnp.bfloat16),
        right_grad,
    )
    alignment_piece, attention_piece, vector_piece, projection_piece = backward_function(
        cotangent_list
    )
    focus_derivative = attention_piece.astype(jnp.float32)
    affine_derivative = vector_piece
    factor_derivative = projection_piece.astype(jnp.float32)
    focus_derivative, affine_derivative, factor_derivative, pair_weight_gradient = lax.psum(
        (focus_derivative, affine_derivative, factor_derivative, pair_weight_gradient),
        ("dp", "axial"),
    )
    return (
        alignment_piece[None],
        focus_derivative,
        affine_derivative,
        factor_derivative,
        pair_weight_gradient,
    )


def solution(mesh):
    return jax.shard_map(
        per_device,
        mesh=mesh,
        in_specs=(
            P("dp", None, "axial", None),
            P("dp", None, "axial", None),
            P("dp", "axial", None, None),
            P("dp", None),
            P("dp", None),
            P(),
            P(),
            P(),
            P(),
        ),
        out_specs=(P("dp", None, "axial", None), P(), P(), P(), P()),
        check_vma=False,
    )
```

profile of v0, /device:TPU:0, one launch (start us, length us, event | category | flops | bytes accessed | tf_op | source)
XLA Modules:
  0.0 220.5 jit_solution(12519017308732594654)
XLA Ops:
  9.4 1.5 fusion.131
  10.9 1.2 fusion.11
  12.1 1.2 convolution_convert_fusion.18
  20.4 1.9 multiply_convert_fusion
  22.3 1.2 fusion.134
  29.5 1.4 multiply_divide_fusion
  30.9 2.0 multiply_maximum_fusion
  32.9 6.3 %all_gather.3 = bf16[32,16,32]{2,1,0:T(8,128)(2,1)S(1)} all-gather(bf16[32,8,32]{2,1,0:T(8,128)(2,1)} %get-tuple-element.8), channel_id=1, replica_groups=mesh['dp'=16,'axial'=2] {'axial'}, dimensions={1}, use_global_device_ids=true | all-gather | bytes 49152 | tf_op jit(solution)/shard_map/all_gather | solution.py:122
  39.9 2.3 %fusion = bf16[8,16,32,32]{2,3,0,1:T(8,128)(2,1)} fusion(bf16[32,16,32,1]{2,1,0,3:T(8,128)(2,1)S(1)} %bitcast.263, bf16[32,8,32]{2,1,0:T(8,128)(2,1)} %copy-done.18), kind=kOutput, calls=%fused_computation.1 | convolution fusion | flops 8519680 | bytes 311296 | tf_op jit(solution)/shard_map/jvp(sic,sje->ijce)/dot_general | solution.py:82
  42.2 1.6 copy.105
  43.8 1.8 convert_element_type.291
  46.5 2.0 fusion.6
  48.5 1.4 convolution_bitcast_fusion.2
  52.9 1.8 fusion.135
  55.6 1.2 fusion.4
  57.9 1.5 fusion.5
  59.4 1.5 fusion.3
  60.9 1.2 fusion.126
  62.1 1.9 copy.96
  65.3 1.2 copy.99
  68.7 1.4 fusion.51
  75.0 41.5 %psum.29 = f32[5,256]{1,0:T(8,128)} all-reduce(f32[5,256]{1,0:T(8,128)S(1)} %pad_add_fusion.3), channel_id=1, replica_groups=mesh['dp'=16,'axial'=2] {'dp','axial'}, use_global_device_ids=true, to_apply=%region_19.0 | all-reduce | flops 1280 | bytes 10240 | tf_op jit(solution)/shard_map/psum | solution.py:146
  117.3 92.3 %all-reduce.15.cloned.1.call-done = (f32[5,256,256]{2,1,0:T(8,128)}, f32[256,64]{0,1:T(8,128)}, f32[1024,128]{1,0:T(8,128)}) async-done(((f32[5,256,256]{2,1,0:T(8,128)}, f32[256,64]{0,1:T(8,128)}, f32[1024,128]{1,0:T(8,128)}), (f32[5,256,256]{2,1,0:T(8,128)}, f32[256,64]{0,1:T(8,128)}, f32[1024,128]{1,0:T(8,128)})) %all-reduce.15.cloned.1.call-update) | async-done | bytes 1900560 | tf_op jit(solution)/shard_map/psum | solution.py:146
  209.7 2.6 %copy.154 = f32[5,256,256]{2,1,0:T(8,128)} copy(f32[5,256,256]{2,1,0:T(8,128)} %get-tuple-element.52) | data formatting | bytes 2621440
  (232 shorter events, 31.3 us)
Async XLA Ops:
  7.2 19.5 %copy-start = (bf16[1024,128]{1,0:T(8,128)(2,1)S(1)}, bf16[1024,128]{1,0:T(8,128)(2,1)}, u32[]{:S(2)}) copy-start(bf16[1024,128]{1,0:T(8,128)(2,1)} %param.17) | copy-start | bytes 786436
  7.2 6.2 %copy-start.1 = (bf16[1,32,8,256]{3,2,1,0:T(8,128)(2,1)S(1)}, bf16[1,32,8,256]{3,2,1,0:T(8,128)(2,1)}, u32[]{:S(2)}) copy-start(bf16[1,32,8,256]{3,2,1,0:T(8,128)(2,1)} %param.9) | copy-start | bytes 393220
  7.2 43.5 %reduce-scatter.4.cloned.1.call-start = ((), (), s32[]{:S(2)}) async-start(), calls=%async_computation.1 | async-start | bytes 49152
  9.4 5.2 %copy-start.27 = (f32[32,8]{1,0:T(8,128)}, f32[32,8]{1,0:T(8,128)S(1)}, u32[]{:S(2)}) copy-start(f32[32,8]{1,0:T(8,128)S(1)} %fusion.48) | copy-start | bytes 3076
  9.4 5.4 %copy-start.38 = (f32[32,8]{1,0:T(8,128)}, f32[32,8]{1,0:T(8,128)S(1)}, u32[]{:S(2)}) copy-start(f32[32,8]{1,0:T(8,128)S(1)} %fusion.115) | copy-start | bytes 3076
  10.9 3.9 %copy-start.53 = (f32[1,256]{1,0:T(1,128)}, f32[1,256]{1,0:T(1,128)S(1)}, u32[]{:S(2)}) copy-start(f32[1,256]{1,0:T(1,128)S(1)} %get-tuple-element.31) | copy-start | bytes 3076
  10.9 3.9 %copy-start.65 = (f32[1,256]{1,0:T(1,128)}, f32[1,256]{1,0:T(1,128)S(1)}, u32[]{:S(2)}) copy-start(f32[1,256]{1,0:T(1,128)S(1)} %get-tuple-element.30) | copy-start | bytes 3076
  20.0 3.8 %copy-start.12 = (f32[256,256]{1,0:T(8,128)}, f32[256,256]{1,0:T(8,128)S(1)}, u32[]{:S(2)}) copy-start(f32[256,256]{1,0:T(8,128)S(1)} %reshape.445) | copy-start | bytes 786436
  20.3 4.3 %copy-start.58 = (f32[1,256]{1,0:T(1,128)S(1)}, f32[1,256]{1,0:T(1,128)}, u32[]{:S(2)}) copy-start(f32[1,256]{1,0:T(1,128)} %get-tuple-element.28) | copy-start | bytes 3076
  20.4 4.3 %copy-start.68 = (f32[1,256]{1,0:T(1,128)S(1)}, f32[1,256]{1,0:T(1,128)}, u32[]{:S(2)}) copy-start(f32[1,256]{1,0:T(1,128)} %get-tuple-element.32) | copy-start | bytes 3076
  20.4 4.3 %copy-start.75 = (bf16[256,64]{0,1:T(8,128)(2,1)S(1)}, bf16[256,64]{0,1:T(8,128)(2,1)}, u32[]{:S(2)}) copy-start(bf16[256,64]{0,1:T(8,128)(2,1)} %param.16) | copy-start | bytes 98308
  22.3 4.4 %copy-start.21 = (bf16[256,256]{1,0:T(8,128)(2,1)}, bf16[256,256]{1,0:T(8,128)(2,1)S(1)}, u32[]{:S(2)}) copy-start(bf16[256,256]{1,0:T(8,128)(2,1)S(1)} %get-tuple-element.39) | copy-start | bytes 393220
  22.3 4.3 %copy-start.36 = (bf16[1,8,16,128]{3,2,1,0:T(8,128)(2,1)S(1)}, bf16[1,8,16,128]{3,2,1,0:T(8,128)(2,1)}, u32[]{:S(2)}) copy-start(bf16[1,8,16,128]{3,2,1,0:T(8,128)(2,1)} %param.11) | copy-start | bytes 98308
  23.8 3.9 %copy-start.64 = (f32[16]{0:T(128)}, f32[16]{0:T(128)S(1)}, u32[]{:S(2)}) copy-start(f32[16]{0:T(128)S(1)} %convert_bitcast_fusion.2) | copy-start | bytes 196
  28.9 180.8 %all-reduce.15.cloned.1.call-start = ((), (), s32[]{:S(2)}) async-start(), calls=%async_computation.2 | async-start | bytes 3801088 | tf_op jit(solution)/shard_map/psum | solution.py:146
  45.6 6.0 %copy-start.3 = (f32[32,8,256]{2,1,0:T(8,128)S(1)}, f32[32,8,256]{2,1,0:T(8,128)}, u32[]{:S(2)}) copy-start(f32[32,8,256]{2,1,0:T(8,128)} %copy-done.2) | copy-start | bytes 786436
  45.6 6.0 %copy-start.30 = (f32[32,8]{1,0:T(8,128)S(1)}, f32[32,8]{1,0:T(8,128)}, u32[]{:S(2)}) copy-start(f32[32,8]{1,0:T(8,128)} %copy-done.29) | copy-start | bytes 3076
  45.6 6.0 %copy-start.47 = (f32[32,8]{1,0:T(8,128)S(1)}, f32[32,8]{1,0:T(8,128)}, u32[]{:S(2)}) copy-start(f32[32,8]{1,0:T(8,128)} %copy-done.46) | copy-start | bytes 3076
  45.6 6.0 %copy-start.51 = (f32[32,8]{1,0:T(8,128)S(1)}, f32[32,8]{1,0:T(8,128)}, u32[]{:S(2)}) copy-start(f32[32,8]{1,0:T(8,128)} %copy-done.50) | copy-start | bytes 3076
  45.6 6.0 %copy-start.59 = (f32[1,256]{1,0:T(1,128)S(1)}, f32[1,256]{1,0:T(1,128)}, u32[]{:S(2)}) copy-start(f32[1,256]{1,0:T(1,128)} %get-tuple-element.28) | copy-start | bytes 3076
  45.6 6.0 %copy-start.76 = (bf16[256,64]{0,1:T(8,128)(2,1)S(1)}, bf16[256,64]{0,1:T(8,128)(2,1)}, u32[]{:S(2)}) copy-start(bf16[256,64]{0,1:T(8,128)(2,1)} %param.16) | copy-start | bytes 98308
  48.5 4.0 %copy-start.26 = (f32[32,8]{1,0:T(8,128)S(1)}, f32[32,8]{1,0:T(8,128)}, u32[]{:S(2)}) copy-start(f32[32,8]{1,0:T(8,128)} %copy-done.25) | copy-start | bytes 3076
  48.5 4.0 %copy-start.48 = (f32[32,8]{1,0:T(8,128)S(1)}, f32[32,8]{1,0:T(8,128)}, u32[]{:S(2)}) copy-start(f32[32,8]{1,0:T(8,128)} %copy-done.46) | copy-start | bytes 3076
  48.5 4.0 %copy-start.60 = (f32[1,256]{1,0:T(1,128)S(1)}, f32[1,256]{1,0:T(1,128)}, u32[]{:S(2)}) copy-start(f32[1,256]{1,0:T(1,128)} %get-tuple-element.28) | copy-start | bytes 3076
  (55 other events, 106.0 us)
Sparse Core Ops, SparseCore 0:
  29.0 12.4 reduce-scatter.3
  74.4 135.1 all-reduce.14
where the time goes:
time: 221 us
  waiting for transfers between devices  92.4 us (42%)
  blocking collectives  47.8 us (22%)
  matrix products  28.2 us (13%)
  local copies, waits for them, and re-layouts  24.5 us (11%)
  between operations  15.2 us (7%)
  other arithmetic  12.4 us (6%)
    psum x1, waiting for transfers between devices, per_device(): lax.psum((focus_derivative, affine_derivative, factor_derivative, pair_we...  92.3 us
    psum x1, blocking collectives, per_device(): lax.psum((focus_derivative, affine_derivative, factor_derivative, pair_we...  41.5 us
    unnamed x160, local copies, waits for them, and re-layouts  9.1 us
    all_gather x1, blocking collectives, per_device(): right_all = lax.all_gather(right_own, 'axial', axis=1, tiled=True)  6.33 us
  transfers between devices with their start and end apart: 2, of which 1 were waited for; matrix products, arithmetic and copies ran while one was open for 7% of the time, Pallas kernels for 0%

commit v1 on v0

--- a/solution.py
+++ b/solution.py
@@ -89,7 +89,55 @@
     return pair_rows / divisor[:, :, None]
 
 
+def exchange(value, axes, total, offset):
+    return lax.ppermute(value, axes, [(i, i ^ offset) for i in range(total)])
+
+
+def reduce_gradients(parts, dp_size, axial_size):
+    axes = ("dp", "axial")
+    if axial_size != 2 or dp_size != 16:
+        return lax.psum(parts, axes)
+    total = dp_size * axial_size
+    flat = jnp.concatenate([p.reshape(-1, 128) for p in parts], axis=0)
+    used = flat.shape[0]
+    rows = -(-used // 128) * 128
+    flat = jnp.pad(flat, ((0, rows - used), (0, 0)))
+    index = lax.axis_index(axes)
+    core = (index // 2) % 2
+    half = rows // 2
+    keep = lax.dynamic_slice_in_dim(flat, core * half, half)
+    send = lax.dynamic_slice_in_dim(flat, (1 - core) * half, half)
+    mine = keep + exchange(send.astype(jnp.bfloat16), axes, total, 2).astype(jnp.float32)
+    place = (index % 2) + 2 * ((index // 4) % 2)
+    offsets = (1, 4, 5)
+    quarter = half // 4
+    own = lax.dynamic_slice_in_dim(mine, place * quarter, quarter)
+    got = []
+    for step, offset in zip((1, 2, 3), offsets):
+        piece = lax.dynamic_slice_in_dim(mine, (place ^ step) * quarter, quarter)
+        got.append(exchange(piece.astype(jnp.bfloat16), axes, total, offset))
+    own = own + got[0].astype(jnp.float32) + got[1].astype(jnp.float32) + got[2].astype(jnp.float32)
+    own = own.astype(jnp.bfloat16)
+    level = [exchange(own, axes, total, offset).astype(jnp.float32) for offset in (8, 16, 24)]
+    own = ((own.astype(jnp.float32) + level[0]) + (level[1] + level[2])).astype(jnp.bfloat16)
+    pieces = [own] + [exchange(own, axes, total, offset) for offset in offsets]
+    stacked = jnp.stack(pieces)
+    mine = jnp.concatenate([lax.dynamic_index_in_dim(stacked, place ^ k, keepdims=False) for k in range(4)], axis=0)
+    other = exchange(mine, axes, total, 2)
+    both = jnp.concatenate(
+        [jnp.where(core == 0, mine, other), jnp.where(core == 0, other, mine)], axis=0
+    ).astype(jnp.float32)
+    outs, at = [], 0
+    for p in parts:
+        n = p.size // 128
+        outs.append(both[at : at + n].reshape(p.shape))
+        at += n
+    return tuple(outs)
+
+
 def per_device(
+    dp_size,
+    axial_size,
     homolog_activations,
     homolog_adjoint,
     duplex_adjoint,
@@ -143,9 +191,10 @@
     focus_derivative = attention_piece.astype(jnp.float32)
     affine_derivative = vector_piece
     factor_derivative = projection_piece.astype(jnp.float32)
-    focus_derivative, affine_derivative, factor_derivative, pair_weight_gradient = lax.psum(
+    focus_derivative, affine_derivative, factor_derivative, pair_weight_gradient = reduce_gradients(
         (focus_derivative, affine_derivative, factor_derivative, pair_weight_gradient),
-        ("dp", "axial"),
+        dp_size,
+        axial_size,
     )
     return (
         alignment_piece[None],
@@ -158,7 +207,7 @@
 
 def solution(mesh):
     return jax.shard_map(
-        per_device,
+        partial(per_device, mesh.shape["dp"], mesh.shape["axial"]),
         mesh=mesh,
         in_specs=(
             P("dp", None, "axial", None),

time: 221 us -> 131 us (0.59)
  waiting for transfers between devices: 92.4 us -> 22.3 us
  blocking collectives: 47.8 us -> 8.18 us
  starting transfers between devices: 0.08 us -> 11.7 us
  local copies, waits for them, and re-layouts: 24.5 us -> 27.2 us
    psum x1 -> x0, waiting for transfers between devices: 92.3 us -> none  [per_device(): lax.psum((focus_derivative, affine_derivative, factor_derivative, pair_we...]
    psum x1 -> x0, blocking collectives: 41.5 us -> none  [per_device(): lax.psum((focus_derivative, affine_derivative, factor_derivative, pair_we...]
    ppermute x0 -> x11, waiting for transfers between devices: none -> 22.3 us  [exchange(): return lax.ppermute(value, axes, [(i, i ^ offset) for i in range(total)])]
    ppermute x0 -> x11, starting transfers between devices: none -> 11.7 us  [exchange(): return lax.ppermute(value, axes, [(i, i ^ offset) for i in range(total)])]
    unnamed x160 -> x168, local copies, waits for them, and re-layouts: 9.1 us -> 3.56 us
    concatenate x0 -> x1, local copies, waits for them, and re-layouts: none -> 3.31 us  [reduce_gradients(): flat = jnp.concatenate([p.reshape(-1, 128) for p in parts], axis=0)]
    reshape x0 -> x7, local copies, waits for them, and re-layouts: none -> 3 us  [the longest x3 2.1 us: reduce_gradients(): outs.append(both[at:at + n].reshape(p.shape))]
  transfers between devices with their start and end apart: 2 -> 12, of which waited for: 1 -> 10; matrix products, arithmetic and copies ran while one was open for 7% -> 12% of each run, Pallas kernels for 0% -> 0%
where the time goes in v1:
time: 131 us; the launch traced here: 130 us
  matrix products  30.4 us (23%)
  local copies, waits for them, and re-layouts  27.2 us (21%)
  waiting for transfers between devices  22.3 us (17%)
  between operations  15.7 us (12%)
  other arithmetic  14.2 us (11%)
  starting transfers between devices  11.7 us (9%)
  blocking collectives  8.18 us (6%)
    ppermute x11, waiting for transfers between devices, exchange(): return lax.ppermute(value, axes, [(i, i ^ offset) for i in range(total)])  22.3 us
    ppermute x11, starting transfers between devices, exchange(): return lax.ppermute(value, axes, [(i, i ^ offset) for i in range(total)])  11.7 us
    all_gather x1, blocking collectives, per_device(): right_all = lax.all_gather(right_own, 'axial', axis=1, tiled=True)  8.18 us
    dot_general x3, matrix products, column_attention_block(): jnp.einsum('rhst,trhd->srhd', probs, values_all, preferred_element_type=j...  4.47 us
    dot_general x3, matrix products, column_attention_block(): jnp.dot(flat_rows, focus_matrices_tier[3], preferred_element_type=jnp.flo...  4.24 us
    dot_general x3, matrix products, pair_block(): jnp.einsum('sic,sje->ijce', left_part, right_part, precision=lax.Precisio...  4.08 us
    unnamed x168, local copies, waits for them, and re-layouts  3.56 us
    dot_general x3, matrix products, column_attention_block(): jnp.dot(gated, focus_matrices_tier[4], preferred_element_type=jnp.float32)  3.53 us
  transfers between devices with their start and end apart: 12, of which 10 were waited for; matrix products, arithmetic and copies ran while one was open for 12% of the time, Pallas kernels for 0%

profile of v1, /device:TPU:0, one launch (start us, length us, event | category | flops | bytes accessed | tf_op | source)
XLA Modules:
  0.0 129.7 jit_solution(4127435759867920737)
XLA Ops:
  17.0 1.5 %convolution_bitcast_fusion = f32[32,8,8,32]{0,3,2,1:T(8,128)} fusion(bf16[32,8,8,32]{3,2,1,0:T(8,128)(2,1)S(1)} %reshape.466, f32[8,8,32,32]{2,3,1,0:T(8,128)S(1)} %get-tuple-element.59, f32[8,8,32]{2,1,0:T(8,128)S(1)} %fusion.38, f32[8,8,32]{2,1,0:T(8,128)S(1)} %get-tuple-element.58), kind=kOutput, calls=%fused_computation.4 | convolution fusion | flops 4390912 | bytes 671744 | tf_op jit(solution)/shard_map/jvp(rhst,trhd->srhd)/dot_general | solution.py:60
  18.5 2.2 %copy.90 = f32[32,8,8,32]{3,2,1,0:T(8,128)S(1)} copy(f32[32,8,8,32]{0,3,2,1:T(8,128)} %convolution_bitcast_fusion) | data formatting | bytes 524288 | tf_op jit(solution)/shard_map/jvp(rhst,trhd->srhd)/transpose | solution.py:60
  21.1 1.9 %multiply_convert_fusion = (bf16[256,256]{1,0:T(8,128)(2,1)S(1)}, f32[256,256]{1,0:T(8,128)}) fusion(f32[256,256]{1,0:T(8,128)S(1)} %reshape.469, f32[256]{0:T(256)S(1)} %bitcast.309, bf16[5,256,256]{2,1,0:T(8,128)(2,1)} %param.14, bf16[1,32,8,256]{3,2,1,0:T(8,128)(2,1)S(1)} %copy-done.3, f32[256]{0:T(256)S(1)} %bitcast.302, f32[256]{0:T(256)S(1)} %bitcast.284, ...), kind=kOutput, calls=%fused_computation.129 | convolution fusion | flops 34340864 | bytes 922624 | tf_op jit(solution)/shard_map/jvp()/dot_general | solution.py:54
  30.5 2.0 %multiply_maximum_fusion = f32[8,16]{1,0:T(8,128)} fusion(f32[]{:T(128)} %get-tuple-element.57, f32[16]{0:T(128)} %copy-done.70, f32[8]{0:T(128)} %copy-done.63), kind=kLoop, calls=%fused_computation.195 | loop fusion | flops 384 | bytes 612 | tf_op jit(solution)/shard_map/jvp()/max | solution.py:88
  32.5 8.2 %all_gather.3 = bf16[32,16,32]{2,1,0:T(8,128)(2,1)} all-gather(bf16[32,8,32]{2,1,0:T(8,128)(2,1)} %get-tuple-element.8), channel_id=1, replica_groups=mesh['dp'=16,'axial'=2] {'axial'}, dimensions={1}, use_global_device_ids=true | all-gather | bytes 49152 | tf_op jit(solution)/shard_map/all_gather | solution.py:170
  40.7 2.3 %fusion = bf16[8,16,32,32]{2,3,0,1:T(8,128)(2,1)} fusion(bf16[32,16,32,1]{2,1,0,3:T(8,128)(2,1)} %bitcast.50, bf16[32,8,32]{2,1,0:T(8,128)(2,1)} %copy-done.26), kind=kOutput, calls=%fused_computation.3 | convolution fusion | flops 8519680 | bytes 311296 | tf_op jit(solution)/shard_map/jvp(sic,sje->ijce)/dot_general | solution.py:82
  43.0 1.6 %copy.110 = bf16[8,16,32,32]{3,2,1,0:T(8,128)(2,1)S(1)} copy(bf16[8,16,32,32]{2,3,0,1:T(8,128)(2,1)} %fusion) | data formatting | bytes 524288 | tf_op jit(solution)/shard_map/jvp()/convert_element_type | solution.py:84
  44.6 1.8 %convert_element_type.332 = bf16[128,1024]{1,0:T(8,128)(2,1)} reshape(bf16[8,16,32,32]{3,2,1,0:T(8,128)(2,1)S(1)} %copy.110) | data formatting | bytes 524288 | tf_op jit(solution)/shard_map/jvp()/convert_element_type | solution.py:84
  47.4 2.0 %fusion.6 = f32[1024,128]{1,0:T(8,128)} fusion(bf16[128,1024]{1,0:T(8,128)(2,1)} %convert_element_type.332, bf16[128,128]{1,0:T(8,128)(2,1)S(1)} %bitcast.277), kind=kOutput, calls=%fused_computation.18 | convolution fusion | flops 33685504 | bytes 819200 | tf_op jit(solution)/shard_map/transpose(jvp())/dot_general | solution.py:85
  53.7 2.0 %fusion.139 = (bf16[256,256]{1,0:T(8,128)(2,1)S(1)}, f32[256,256]{1,0:T(8,128)}) fusion(f32[256,256]{1,0:T(8,128)} %get-tuple-element.61, bf16[5,256,256]{2,1,0:T(8,128)(2,1)} %param.14, f32[32,8]{1,0:T(8,128)S(1)} %negate_multiply_fusion, f32[32,8,256]{2,1,0:T(8,128)S(1)} %get-tuple-element.33, bf16[1,32,8,256]{3,2,1,0:T(8,128)(2,1)S(1)} %copy-done.15), kind=kOutput, calls=%fused_computation.217 | convolution fusion | flops 34013184 | bytes 1180672 | tf_op jit(solution)/shard_map/transpose(jvp())/dot_general | solution.py:64
  57.4 1.7 %fusion.31 = (f32[8,8,32]{2,1,0:T(8,128)S(1)}, bf16[8,8,32,32]{2,3,1,0:T(8,128)(2,1)S(1)}) fusion(f32[8,8,32,32]{2,3,1,0:T(8,128)S(1)} %get-tuple-element.59, f32[8,8,32]{2,1,0:T(8,128)} %multiply_divide_fusion, f32[8,8,32]{2,1,0:T(8,128)} %copy-done.29, bf16[32,8,8,32]{3,2,1,0:T(8,128)(2,1)S(1)} %copy-done.13, bf16[32,8,8,32]{0,3,2,1:T(8,128)(2,1)} %copy.98), kind=kOutput, calls=%fused_computation.64 | convolution fusion | flops 4519936 | bytes 679936 | tf_op jit(solution)/shard_map/transpose(jvp(rhst,trhd->srhd))/dot_general | solution.py:60
  60.2 1.5 %fusion.5 = bf16[32,8,8,32]{3,0,2,1:T(8,128)(2,1)} fusion(bf16[32,8,8,32]{3,2,1,0:T(8,128)(2,1)S(1)} %copy-done.11, bf16[8,8,32,32]{2,3,1,0:T(8,128)(2,1)S(1)} %get-tuple-element.68, f32[8,8,32,32]{2,3,1,0:T(8,128)S(1)} %get-tuple-element.59, f32[8,8,32]{2,1,0:T(8,128)S(1)} %neg.17, f32[8,8,32]{2,1,0:T(8,128)S(1)} %copy-done.42, f32[8,8,32]{2,1,0:T(8,128)S(1)} %copy-done.30), kind=kOutput, calls=%fused_computation.16 | convolution fusion | flops 4587520 | bytes 679936 | tf_op jit(solution)/shard_map/transpose(jvp(srhd,trhd->rhst))/dot_general | solution.py:57
  67.0 1.9 %copy.100 = bf16[32,8,8,32]{3,2,1,0:T(8,128)(2,1)S(1)} copy(bf16[32,8,8,32]{0,3,2,1:T(8,128)(2,1)} %fusion.4) | data formatting | bytes 262144 | tf_op jit(solution)/shard_map/transpose(jvp(rhst,trhd->srhd))/convert_element_type | solution.py:60
  70.2 2.0 %fusion.53 = (f32[256]{0:T(256)}, f32[32,8]{1,0:T(8,128)S(1)}, f32[256,256]{1,0:T(8,128)S(1)}) fusion(bf16[1,32,8,256]{3,2,1,0:T(8,128)(2,1)S(1)} %copy-done.3, f32[32,8]{1,0:T(8,128)S(1)} %copy-done.45, f32[32,8]{1,0:T(8,128)S(1)} %copy-done.32, f32[256]{0:T(256)S(1)} %bitcast.285, bf16[256,256]{1,0:T(8,128)(2,1)} %convolution_convert_fusion.10, ...), kind=kOutput, calls=%fused_computation.102 | convolution fusion | flops 34340352 | bytes 1084416 | tf_op jit(solution)/shard_map/transpose(jvp())/dot_general | solution.py:54
  78.3 3.3 %concatenate.9 = f32[3722,128]{1,0:T(8,128)S(1)} concatenate(f32[2560,128]{1,0:T(8,128)S(1)} %reshape.491, f32[10,128]{1,0:T(8,128)S(1)} %reshape.479, f32[128,128]{1,0:T(8,128)} %reshape.493, f32[1024,128]{1,0:T(8,128)} %fusion.6), dimensions={0} | concatenate | bytes 3811328 | tf_op jit(solution)/shard_map/concatenate | solution.py:101
  82.0 1.9 %collective-permute-done = bf16[1920,128]{1,0:T(8,128)(2,1)} collective-permute-done((bf16[1920,128]{1,0:T(8,128)(2,1)S(1)}, bf16[1920,128]{1,0:T(8,128)(2,1)}, u32[]{:S(2)}, u32[]{:S(2)}) %collective-permute-start) | collective-permute-done | bytes 491552 | tf_op jit(solution)/shard_map/ppermute | solution.py:93
  85.2 1.6 %collective-permute-start.3 = (bf16[480,128]{1,0:T(8,128)(2,1)S(1)}, bf16[480,128]{1,0:T(8,128)(2,1)S(1)}, u32[]{:S(2)}, u32[]{:S(2)}) collective-permute-start(bf16[480,128]{1,0:T(8,128)(2,1)S(1)} %get-tuple-element.39), channel_id=1, source_target_pairs={{0,5},{1,4},{2,7},{3,6},{4,1},{5,0},{6,3},{7,2},{8,13},{9,12},{10,... | collective-permute-start | bytes 368648 | tf_op jit(solution)/shard_map/ppermute | solution.py:93
  87.3 1.5 %collective-permute-start.1 = (bf16[480,128]{1,0:T(8,128)(2,1)S(1)}, bf16[480,128]{1,0:T(8,128)(2,1)S(1)}, u32[]{:S(2)}, u32[]{:S(2)}) collective-permute-start(bf16[480,128]{1,0:T(8,128)(2,1)S(1)} %get-tuple-element.38), channel_id=1, source_target_pairs={{0,1},{1,0},{2,3},{3,2},{4,5},{5,4},{6,7},{7,6},{8,9},{9,8},{10,11... | collective-permute-start | bytes 368648 | tf_op jit(solution)/shard_map/ppermute | solution.py:93
  88.8 3.6 %collective-permute-done.3 = bf16[480,128]{1,0:T(8,128)(2,1)S(1)} collective-permute-done((bf16[480,128]{1,0:T(8,128)(2,1)S(1)}, bf16[480,128]{1,0:T(8,128)(2,1)S(1)}, u32[]{:S(2)}, u32[]{:S(2)}) %collective-permute-start.3) | collective-permute-done | bytes 122912 | tf_op jit(solution)/shard_map/ppermute | solution.py:93
  94.3 3.7 %collective-permute-start.6 = (bf16[480,128]{1,0:T(8,128)(2,1)S(1)}, bf16[480,128]{1,0:T(8,128)(2,1)S(1)}, u32[]{:S(2)}, u32[]{:S(2)}) collective-permute-start(bf16[480,128]{1,0:T(8,128)(2,1)S(1)} %add_convert_fusion.3), channel_id=1, source_target_pairs={{0,24},{1,25},{2,26},{3,27},{4,28},{5,29},{6,30},{7,31},{8,16},{9,... | collective-permute-start | bytes 368648 | tf_op jit(solution)/shard_map/ppermute | solution.py:93
  98.8 3.7 %collective-permute-done.6 = bf16[480,128]{1,0:T(8,128)(2,1)S(1)} collective-permute-done((bf16[480,128]{1,0:T(8,128)(2,1)S(1)}, bf16[480,128]{1,0:T(8,128)(2,1)S(1)}, u32[]{:S(2)}, u32[]{:S(2)}) %collective-permute-start.6) | collective-permute-done | bytes 122912 | tf_op jit(solution)/shard_map/ppermute | solution.py:93
  102.4 6.1 %collective-permute-done.5 = bf16[480,128]{1,0:T(8,128)(2,1)S(1)} collective-permute-done((bf16[480,128]{1,0:T(8,128)(2,1)S(1)}, bf16[480,128]{1,0:T(8,128)(2,1)S(1)}, u32[]{:S(2)}, u32[]{:S(2)}) %collective-permute-start.5) | collective-permute-done | bytes 122912 | tf_op jit(solution)/shard_map/ppermute | solution.py:93
  110.2 2.0 %collective-permute-start.7 = (bf16[480,128]{1,0:T(8,128)(2,1)S(1)}, bf16[480,128]{1,0:T(8,128)(2,1)S(1)}, u32[]{:S(2)}, u32[]{:S(2)}) collective-permute-start(bf16[480,128]{1,0:T(8,128)(2,1)S(1)} %add_convert_fusion.2), channel_id=1, source_target_pairs={{0,1},{1,0},{2,3},{3,2},{4,5},{5,4},{6,7},{7,6},{8,9},{9,8},{10,11... | collective-permute-start | bytes 368648 | tf_op jit(solution)/shard_map/ppermute | solution.py:93
  112.1 3.2 %collective-permute-done.9 = bf16[480,128]{1,0:T(8,128)(2,1)S(1)} collective-permute-done((bf16[480,128]{1,0:T(8,128)(2,1)S(1)}, bf16[480,128]{1,0:T(8,128)(2,1)S(1)}, u32[]{:S(2)}, u32[]{:S(2)}) %collective-permute-start.9) | collective-permute-done | bytes 122912 | tf_op jit(solution)/shard_map/ppermute | solution.py:93
  (280 shorter events, 51.0 us)
Async XLA Ops:
  7.2 18.8 %copy-start = (bf16[1024,128]{1,0:T(8,128)(2,1)S(1)}, bf16[1024,128]{1,0:T(8,128)(2,1)}, u32[]{:S(2)}) copy-start(bf16[1024,128]{1,0:T(8,128)(2,1)} %param.17) | copy-start | bytes 786436
  7.2 44.4 %reduce-scatter.4.cloned.1.call-start = ((), (), s32[]{:S(2)}) async-start(), calls=%async_computation.1 | async-start | bytes 49152
  8.3 42.6 %copy-start.31 = (f32[32,8]{1,0:T(8,128)}, f32[32,8]{1,0:T(8,128)S(1)}, u32[]{:S(2)}) copy-start(f32[32,8]{1,0:T(8,128)S(1)} %broadcast_multiply_fusion.1) | copy-start | bytes 3076
  10.3 16.7 %copy-start.64 = (f32[1,256]{1,0:T(1,128)}, f32[1,256]{1,0:T(1,128)S(1)}, u32[]{:S(2)}) copy-start(f32[1,256]{1,0:T(1,128)S(1)} %get-tuple-element.49) | copy-start | bytes 3076
  10.3 16.7 %copy-start.74 = (f32[1,256]{1,0:T(1,128)}, f32[1,256]{1,0:T(1,128)S(1)}, u32[]{:S(2)}) copy-start(f32[1,256]{1,0:T(1,128)S(1)} %get-tuple-element.53) | copy-start | bytes 3076
  53.7 20.4 %copy-start.1 = (f32[32,8,256]{2,1,0:T(8,128)}, f32[32,8,256]{2,1,0:T(8,128)S(1)}, u32[]{:S(2)}) copy-start(f32[32,8,256]{2,1,0:T(8,128)S(1)} %get-tuple-element.33) | copy-start | bytes 786436
  81.8 2.1 %collective-permute-start = (bf16[1920,128]{1,0:T(8,128)(2,1)S(1)}, bf16[1920,128]{1,0:T(8,128)(2,1)}, u32[]{:S(2)}, u32[]{:S(2)}) collective-permute-start(bf16[1920,128]{1,0:T(8,128)(2,1)S(1)} %fusion.37), channel_id=1, source_target_pairs={{0,2},{1,3},{2,0},{3,1},{4,6},{5,7},{6,4},{7,5},{8,10},{9,11},{10,... | collective-permute-start | bytes 1474568 | tf_op jit(solution)/shard_map/ppermute | solution.py:93
  85.2 7.1 %collective-permute-start.3 = (bf16[480,128]{1,0:T(8,128)(2,1)S(1)}, bf16[480,128]{1,0:T(8,128)(2,1)S(1)}, u32[]{:S(2)}, u32[]{:S(2)}) collective-permute-start(bf16[480,128]{1,0:T(8,128)(2,1)S(1)} %get-tuple-element.39), channel_id=1, source_target_pairs={{0,5},{1,4},{2,7},{3,6},{4,1},{5,0},{6,3},{7,2},{8,13},{9,12},{10,... | collective-permute-start | bytes 368648 | tf_op jit(solution)/shard_map/ppermute | solution.py:93
  86.8 6.5 %collective-permute-start.2 = (bf16[480,128]{1,0:T(8,128)(2,1)S(1)}, bf16[480,128]{1,0:T(8,128)(2,1)S(1)}, u32[]{:S(2)}, u32[]{:S(2)}) collective-permute-start(bf16[480,128]{1,0:T(8,128)(2,1)S(1)} %get-tuple-element.40), channel_id=1, source_target_pairs={{0,4},{1,5},{2,6},{3,7},{4,0},{5,1},{6,2},{7,3},{8,12},{9,13},{10,... | collective-permute-start | bytes 368648 | tf_op jit(solution)/shard_map/ppermute | solution.py:93
  87.3 6.9 %collective-permute-start.1 = (bf16[480,128]{1,0:T(8,128)(2,1)S(1)}, bf16[480,128]{1,0:T(8,128)(2,1)S(1)}, u32[]{:S(2)}, u32[]{:S(2)}) collective-permute-start(bf16[480,128]{1,0:T(8,128)(2,1)S(1)} %get-tuple-element.38), channel_id=1, source_target_pairs={{0,1},{1,0},{2,3},{3,2},{4,5},{5,4},{6,7},{7,6},{8,9},{9,8},{10,11... | collective-permute-start | bytes 368648 | tf_op jit(solution)/shard_map/ppermute | solution.py:93
  94.2 22.7 %copy-start.2 = (f32[32,8,256]{2,1,0:T(8,128)S(1)}, f32[32,8,256]{2,1,0:T(8,128)}, u32[]{:S(2)}) copy-start(f32[32,8,256]{2,1,0:T(8,128)} %copy-done.1) | copy-start | bytes 786436
  94.2 22.7 %copy-start.5 = (bf16[1,32,8,256]{3,2,1,0:T(8,128)(2,1)S(1)}, bf16[1,32,8,256]{3,2,1,0:T(8,128)(2,1)}, u32[]{:S(2)}) copy-start(bf16[1,32,8,256]{3,2,1,0:T(8,128)(2,1)} %param.9) | copy-start | bytes 393220
  94.2 22.7 %copy-start.17 = (bf16[1,32,8,256]{3,2,1,0:T(8,128)(2,1)S(1)}, bf16[1,32,8,256]{3,2,1,0:T(8,128)(2,1)}, u32[]{:S(2)}) copy-start(bf16[1,32,8,256]{3,2,1,0:T(8,128)(2,1)} %param.10) | copy-start | bytes 393220
  94.3 22.7 %copy-start.19 = (f32[256,256]{1,0:T(8,128)S(1)}, f32[256,256]{1,0:T(8,128)}, u32[]{:S(2)}) copy-start(f32[256,256]{1,0:T(8,128)} %copy-done.18) | copy-start | bytes 786436
  94.3 22.7 %copy-start.33 = (f32[32,8]{1,0:T(8,128)S(1)}, f32[32,8]{1,0:T(8,128)}, u32[]{:S(2)}) copy-start(f32[32,8]{1,0:T(8,128)} %copy-done.31) | copy-start | bytes 3076
  94.3 22.7 %copy-start.46 = (f32[32,8]{1,0:T(8,128)S(1)}, f32[32,8]{1,0:T(8,128)}, u32[]{:S(2)}) copy-start(f32[32,8]{1,0:T(8,128)} %copy-done.44) | copy-start | bytes 3076
  94.3 22.7 %copy-start.47 = (f32[32,8]{1,0:T(8,128)S(1)}, f32[32,8]{1,0:T(8,128)}, u32[]{:S(2)}) copy-start(f32[32,8]{1,0:T(8,128)} %get-tuple-element.47) | copy-start | bytes 3076
  94.3 8.1 %collective-permute-start.6 = (bf16[480,128]{1,0:T(8,128)(2,1)S(1)}, bf16[480,128]{1,0:T(8,128)(2,1)S(1)}, u32[]{:S(2)}, u32[]{:S(2)}) collective-permute-start(bf16[480,128]{1,0:T(8,128)(2,1)S(1)} %add_convert_fusion.3), channel_id=1, source_target_pairs={{0,24},{1,25},{2,26},{3,27},{4,28},{5,29},{6,30},{7,31},{8,16},{9,... | collective-permute-start | bytes 368648 | tf_op jit(solution)/shard_map/ppermute | solution.py:93
  98.0 10.5 %collective-permute-start.5 = (bf16[480,128]{1,0:T(8,128)(2,1)S(1)}, bf16[480,128]{1,0:T(8,128)(2,1)S(1)}, u32[]{:S(2)}, u32[]{:S(2)}) collective-permute-start(bf16[480,128]{1,0:T(8,128)(2,1)S(1)} %add_convert_fusion.3), channel_id=1, source_target_pairs={{0,16},{1,17},{2,18},{3,19},{4,20},{5,21},{6,22},{7,23},{8,24},{9,... | collective-permute-start | bytes 368648 | tf_op jit(solution)/shard_map/ppermute | solution.py:93
  98.0 10.5 %collective-permute-start.4 = (bf16[480,128]{1,0:T(8,128)(2,1)S(1)}, bf16[480,128]{1,0:T(8,128)(2,1)S(1)}, u32[]{:S(2)}, u32[]{:S(2)}) collective-permute-start(bf16[480,128]{1,0:T(8,128)(2,1)S(1)} %add_convert_fusion.3), channel_id=1, source_target_pairs={{0,8},{1,9},{2,10},{3,11},{4,12},{5,13},{6,14},{7,15},{8,0},{9,1},... | collective-permute-start | bytes 368648 | tf_op jit(solution)/shard_map/ppermute | solution.py:93
  108.6 6.7 %collective-permute-start.9 = (bf16[480,128]{1,0:T(8,128)(2,1)S(1)}, bf16[480,128]{1,0:T(8,128)(2,1)S(1)}, u32[]{:S(2)}, u32[]{:S(2)}) collective-permute-start(bf16[480,128]{1,0:T(8,128)(2,1)S(1)} %add_convert_fusion.2), channel_id=1, source_target_pairs={{0,5},{1,4},{2,7},{3,6},{4,1},{5,0},{6,3},{7,2},{8,13},{9,12},{10,... | collective-permute-start | bytes 368648 | tf_op jit(solution)/shard_map/ppermute | solution.py:93
  109.7 5.7 %collective-permute-start.8 = (bf16[480,128]{1,0:T(8,128)(2,1)S(1)}, bf16[480,128]{1,0:T(8,128)(2,1)S(1)}, u32[]{:S(2)}, u32[]{:S(2)}) collective-permute-start(bf16[480,128]{1,0:T(8,128)(2,1)S(1)} %add_convert_fusion.2), channel_id=1, source_target_pairs={{0,4},{1,5},{2,6},{3,7},{4,0},{5,1},{6,2},{7,3},{8,12},{9,13},{10,... | collective-permute-start | bytes 368648 | tf_op jit(solution)/shard_map/ppermute | solution.py:93
  110.2 6.4 %collective-permute-start.7 = (bf16[480,128]{1,0:T(8,128)(2,1)S(1)}, bf16[480,128]{1,0:T(8,128)(2,1)S(1)}, u32[]{:S(2)}, u32[]{:S(2)}) collective-permute-start(bf16[480,128]{1,0:T(8,128)(2,1)S(1)} %add_convert_fusion.2), channel_id=1, source_target_pairs={{0,1},{1,0},{2,3},{3,2},{4,5},{5,4},{6,7},{7,6},{8,9},{9,8},{10,11... | collective-permute-start | bytes 368648 | tf_op jit(solution)/shard_map/ppermute | solution.py:93
  116.8 1.9 %collective-permute-start.10 = (bf16[1920,128]{1,0:T(8,128)(2,1)S(1)}, bf16[1920,128]{1,0:T(8,128)(2,1)S(1)}, u32[]{:S(2)}, u32[]{:S(2)}) collective-permute-start(bf16[1920,128]{1,0:T(8,128)(2,1)S(1)} %pad_maximum_fusion.1), channel_id=1, source_target_pairs={{0,2},{1,3},{2,0},{3,1},{4,6},{5,7},{6,4},{7,5},{8,10},{9,11},{10,... | collective-permute-start | bytes 1474568 | tf_op jit(solution)/shard_map/ppermute | solution.py:93
  (70 other events, 275.0 us)
Sparse Core Ops, SparseCore 0:
  29.3 12.4 reduce-scatter.3

commit v2 on v0

v2 whole, which is shorter than its diff:
```python
from functools import partial

import jax
import jax.numpy as jnp
from jax import lax
from jax.experimental import pallas as pl
from jax.experimental.pallas import tpu as pltpu
from jax.sharding import PartitionSpec as P

HEADS = 8
HEAD_DIM = 32
OUTER_FACTORS = 32
DUPLEX_FEATURES = 128
BF = jnp.bfloat16
F32 = jnp.float32


def mm(a, b):
    return lax.dot_general(a, b, (((1,), (0,)), ((), ())), preferred_element_type=F32)


def mm_nt(a, b):
    return lax.dot_general(a, b, (((1,), (1,)), ((), ())), preferred_element_type=F32)


def mm_tn(a, b):
    return lax.dot_general(a, b, (((0,), (0,)), ((), ())), preferred_element_type=F32)


def ids(shape):
    return lax.broadcasted_iota(jnp.int32, shape, 0), lax.broadcasted_iota(jnp.int32, shape, 1)


def ones_where(mask):
    return jnp.where(mask, 1.0, 0.0).astype(BF)


def to_residue_major(seqs, rows):
    r, c = ids((seqs * rows, seqs * rows))
    return ones_where((r // seqs == c % rows) & (r % seqs == c // rows))


def normal_parts(value):
    mean = jnp.mean(value, axis=-1, keepdims=True)
    centered = value - mean
    spread = jnp.mean(centered * centered, axis=-1, keepdims=True)
    scale = lax.rsqrt(spread + 1e-05)
    return centered * scale, scale


def normal_back(cot, hat, scale):
    first = jnp.mean(cot, axis=-1, keepdims=True)
    second = jnp.mean(cot * hat, axis=-1, keepdims=True)
    return scale * (cot - first - hat * second)


def group_max(value):
    halves = []
    for h in range(2):
        x = value[:, h * 128 : (h + 1) * 128]
        lane = lax.broadcasted_iota(jnp.int32, x.shape, 1) % HEAD_DIM
        for shift in (1, 2, 4, 8, 16):
            low = pltpu.roll(x, shift, 1)
            high = pltpu.roll(x, 128 - HEAD_DIM + shift, 1)
            x = jnp.maximum(x, jnp.where(lane >= shift, low, high))
        halves.append(x)
    return jnp.concatenate(halves, axis=1)


def group_sum(value, same):
    high = value.astype(BF)
    low = (value - high.astype(F32)).astype(BF)
    return mm(high, same) + mm(low, same)


def head_mask(width):
    r, c = ids((width, width))
    return r // HEAD_DIM == c // HEAD_DIM


def spread_heads(block, mask):
    return jnp.where(mask, jnp.concatenate([block] * HEADS, axis=0), jnp.zeros((), block.dtype))


def gather_heads(value, mask):
    width = value.shape[1]
    kept = jnp.where(mask, value, 0.0)
    return jnp.sum(kept.reshape(HEADS, width // HEADS, width), axis=0)


def forward_kernel(
    where_ref, x_ref, dup_ref, seq_ref, res_ref, w_ref, aff_ref, lrt_ref,
    proj_ref, pairs_ref, nb_ref, q_ref, k_ref, v_ref, gate_ref, att_ref, p_ref, gated_ref,
    hat1_ref, rs1_ref, hat2_ref, rs2_ref, sec_ref, dup_scr, *, n,
):
    own = where_ref[0]
    seqs = seq_ref.shape[1]
    total = x_ref.shape[0]
    rows = total // seqs
    width = x_ref.shape[1]
    mask = head_mask(width)
    same = ones_where(mask)
    seq_f = seq_ref[...].astype(F32)
    res_f = res_ref[...].astype(F32)
    pair_rows = dup_ref.shape[0]
    sites = pair_rows // rows
    r, c = ids((pair_rows, pair_rows))
    swap = ones_where((r // rows == c % sites) & (r % rows == c // sites))
    dup = mm(swap, dup_ref[...])
    r, c = ids((pair_rows, sites))
    flag_j = jnp.sum(jnp.where(c == r // rows, res_f, 0.0), axis=1, keepdims=True)
    flag_i = jnp.sum(jnp.where(c == r % rows + own * rows, res_f, 0.0), axis=1, keepdims=True)
    present = jnp.sum(seq_f, axis=1, keepdims=True)
    dup_scr[...] = dup / jnp.maximum(flag_i * flag_j * present, 1.0)
    block = rows * rows
    for m in range(n):
        at = lax.rem(own + m, n) * block
        pairs_ref[m * block : (m + 1) * block, :] = dup_scr[pl.ds(pl.multiple_of(at, block), block), :].astype(BF)
    x = mm(to_residue_major(seqs, rows), x_ref[...])
    hat1, rs1 = normal_parts(x)
    hat1_ref[...] = hat1
    rs1_ref[...] = rs1
    nb = (hat1 * aff_ref[0:1, :] + aff_ref[1:2, :]).astype(BF)
    nb_ref[...] = nb
    q = (mm(nb, w_ref[0]) * HEAD_DIM ** (-0.5)).astype(BF)
    k = mm(nb, w_ref[1]).astype(BF)
    v = mm(nb, w_ref[2]).astype(BF)
    q_ref[...] = q
    k_ref[...] = k
    v_ref[...] = v
    gate = jax.nn.sigmoid(mm(nb, w_ref[3]) + aff_ref[2:3, :])
    gate_ref[...] = gate
    r, c = ids((seqs, width))
    over_t = ones_where(r == c % seqs)
    seq8 = jnp.broadcast_to(seq_f, (8, seqs)).astype(BF)
    seq_row = mm(seq8, over_t)[0:1, :]
    logits = []
    for i in range(rows):
        at = slice(i * seqs, (i + 1) * seqs)
        logits.append(mm_nt(q[at], spread_heads(k[at], mask)))
    s = jnp.concatenate(logits, axis=0) + (seq_row - 1.0) * 1000000000.0
    e = jnp.exp(s - group_max(s))
    p = e / group_sum(e, same)
    p_ref[...] = p
    pb = p.astype(BF)
    att = []
    for i in range(rows):
        at = slice(i * seqs, (i + 1) * seqs)
        att.append(mm(pb[at], spread_heads(v[at], mask)))
    att = jnp.concatenate(att, axis=0)
    att_ref[...] = att
    gated = (att * gate).astype(BF)
    gated_ref[...] = gated
    hat2, rs2 = normal_parts(x + mm(gated, w_ref[4]))
    hat2_ref[...] = hat2
    rs2_ref[...] = rs2
    sec = (hat2 * aff_ref[3:4, :] + aff_ref[4:5, :]).astype(BF)
    sec_ref[...] = sec
    proj = mm_nt(lrt_ref[...], sec)
    r, c = ids((sites, total))
    over_r = ones_where(r == c // seqs + own * rows)
    res8 = jnp.broadcast_to(res_f, (8, sites)).astype(BF)
    flags = seq_row * mm(res8, over_r)[0:1, :]
    proj_ref[...] = (proj * flags).astype(BF)


def stack_right(right_t):
    return jnp.concatenate([right_t[:, :128], right_t[:, 128:]], axis=0)


def spread_left(left_t, seqs):
    factors, total = left_t.shape
    lanes = factors * 32
    r, c = ids((factors, lanes))
    pick = ones_where(c // 32 == r)
    r, c = ids((total, lanes))
    held = jnp.where(r // seqs == c % 8, mm_tn(left_t, pick), 0.0).astype(BF)
    r, c = ids((128, total))
    out = mm(ones_where(r % seqs == c % seqs), held)
    r, c = ids((128, lanes))
    return jnp.where(r // seqs == (c // 8) % 4, out, 0.0).astype(BF)


def diagonal(panel):
    zero = jnp.zeros_like(panel)
    return jnp.concatenate(
        [jnp.concatenate([panel if b == a else zero for b in range(4)], axis=1) for a in range(4)], axis=0
    )


def pair_cotangent(wide, diag):
    d = mm_nt(wide, diag).astype(BF)
    return jnp.concatenate([d[g * 32 : (g + 1) * 32] for g in range(8)], axis=1)


def backward_kernel(
    where_ref, proj_ref, pairs_ref, other_proj_ref, other_pairs_ref, wf_ref, adj_ref, seq_ref, res_ref, w_ref, aff_ref,
    lrt_ref, nb_ref, q_ref, k_ref, v_ref, gate_ref, att_ref, p_ref, gated_ref, hat1_ref, rs1_ref,
    hat2_ref, rs2_ref, sec_ref,
    dx_ref, keep_ref, send_ref, grad_scr, *, n,
):
    own, core = where_ref[0], where_ref[1]
    seqs = seq_ref.shape[1]
    total, width = adj_ref.shape
    rows = total // seqs
    block = rows * rows
    factors = OUTER_FACTORS
    mask = head_mask(width)
    same = ones_where(mask)
    seq_f = seq_ref[...].astype(F32)
    res_f = res_ref[...].astype(F32)
    sites = res_ref.shape[1]

    wide = jnp.concatenate(
        [
            jnp.concatenate([wf_ref[g * 128 + b * 32 : g * 128 + (b + 1) * 32, :] for g in range(8)], axis=0)
            for b in range(4)
        ],
        axis=1,
    )
    rights, lefts = [], []
    for m in range(n):
        both = proj_ref[...] if m == 0 else other_proj_ref[m - 1]
        lefts.append(spread_left(both[:factors], seqs))
        rights.append(stack_right(both[factors:]))
    right = jnp.concatenate(rights, axis=0)
    diags = [diagonal(pairs_ref[g * 32 : (g + 1) * 32, :]) for g in range(2 * n)]
    cots = [pair_cotangent(wide, d) for d in diags]
    back = mm_tn(right, jnp.concatenate(cots, axis=0))
    r, c = ids(back.shape)
    back = jnp.where(r // seqs == (c // 8) % 4, back, 0.0)
    back = jnp.sum(back.reshape(4, seqs, back.shape[1]), axis=0)
    tiles = []
    for g in range(8):
        t = back[:, g * 128 : (g + 1) * 128]
        t = t + pltpu.roll(t, 8, 1)
        tiles.append(t + pltpu.roll(t, 16, 1))
    back = jnp.concatenate(tiles, axis=1).astype(BF)
    r, c = ids((total, back.shape[1]))
    back = jnp.where(c % 32 == 24 + r // seqs, jnp.concatenate([back] * rows, axis=0), jnp.zeros((), BF))
    r, c = ids((factors, back.shape[1]))
    left_cot = mm_nt(ones_where(c // 32 == r), back)
    right_cot = mm_nt(jnp.concatenate(cots[:2], axis=0), lefts[0])
    for m in range(1, n):
        inward = [
            pair_cotangent(wide, diagonal(other_pairs_ref[(m - 1) * block + g * 32 : (m - 1) * block + (g + 1) * 32, :]))
            for g in range(2)
        ]
        right_cot = right_cot + mm_nt(jnp.concatenate(inward, axis=0), lefts[m])
    right_cot = right_cot.astype(BF).astype(F32)
    right_cot = jnp.concatenate([right_cot[:factors], right_cot[factors:]], axis=1)
    outer = mm(right, lefts[0]).astype(BF)
    final = jnp.zeros((256, 512), F32)
    for g in range(2 * n):
        o = outer[g * 32 : (g + 1) * 32]
        o = jnp.concatenate([o[:, b * 128 : (b + 1) * 128] for b in range(8)], axis=0)
        final = final + mm(o, diags[g])
    base = 10 * total
    for g in range(8):
        for b in range(4):
            at = base + (4 * g + b) * 32
            grad_scr[at : at + 32, :] = final[g * 32 : (g + 1) * 32, b * 128 : (b + 1) * 128].astype(BF)

    r, c = ids((seqs, total))
    seq_row = mm(jnp.broadcast_to(seq_f, (8, seqs)).astype(BF), ones_where(r == c % seqs))[0:1, :]
    r, c = ids((sites, total))
    res_row = mm(jnp.broadcast_to(res_f, (8, sites)).astype(BF), ones_where(r == c // seqs + own * rows))[0:1, :]
    proj_cot = (jnp.concatenate([left_cot, right_cot], axis=0) * (seq_row * res_row)).astype(BF)
    base = base + 1024
    lr_grad = mm(proj_cot, sec_ref[...]).astype(BF)
    grad_scr[base : base + 64, :] = lr_grad[:, :128]
    grad_scr[base + 64 : base + 128, :] = lr_grad[:, 128:]
    base = base + 128
    turn = to_residue_major(seqs, rows)
    cot = mm_tn(proj_cot, lrt_ref[...]).astype(BF).astype(F32)
    hat2 = hat2_ref[...]
    d_gain2 = jnp.sum(cot * hat2, axis=0, keepdims=True)
    d_bias2 = jnp.sum(cot, axis=0, keepdims=True)
    upd = mm(turn, adj_ref[...]) + normal_back(cot * aff_ref[3:4, :], hat2, rs2_ref[...])

    def put(index, grad):
        grad = grad.astype(BF)
        grad_scr[2 * index * total : (2 * index + 1) * total, :] = grad[:, :128]
        grad_scr[(2 * index + 1) * total : (2 * index + 2) * total, :] = grad[:, 128:]

    upd_b = upd.astype(BF)
    d_gated = mm_nt(upd_b, w_ref[4]).astype(BF).astype(F32)
    put(4, mm_tn(gated_ref[...], upd_b))
    gate = gate_ref[...]
    d_att = d_gated * gate
    d_z = d_gated * att_ref[...] * gate * (1.0 - gate)
    d_gate_bias = jnp.sum(d_z, axis=0, keepdims=True)
    nb = nb_ref[...]
    d_zb = d_z.astype(BF)
    put(3, mm_tn(nb, d_zb))
    d_attb = d_att.astype(BF)
    p = p_ref[...]
    pb = p.astype(BF)
    d_p, d_v = [], []
    for i in range(rows):
        at = slice(i * seqs, (i + 1) * seqs)
        d_p.append(mm_nt(d_attb[at], spread_heads(v_ref[at, :], mask)))
        d_v.append(gather_heads(mm_tn(pb[at], d_attb[at]), mask))
    d_p = jnp.concatenate(d_p, axis=0).astype(BF).astype(F32)
    d_v = jnp.concatenate(d_v, axis=0).astype(BF)
    put(2, mm_tn(nb, d_v))
    d_s = (p * (d_p - group_sum(p * d_p, same))).astype(BF)
    d_q, d_k = [], []
    for i in range(rows):
        at = slice(i * seqs, (i + 1) * seqs)
        d_q.append(mm(d_s[at], spread_heads(k_ref[at, :], mask)))
        d_k.append(gather_heads(mm_tn(d_s[at], q_ref[at, :]), mask))
    d_q = jnp.concatenate(d_q, axis=0).astype(BF).astype(F32) * HEAD_DIM ** (-0.5)
    d_q = d_q.astype(BF)
    d_k = jnp.concatenate(d_k, axis=0).astype(BF)
    put(0, mm_tn(nb, d_q))
    put(1, mm_tn(nb, d_k))
    cot = mm_nt(d_q, w_ref[0]) + mm_nt(d_k, w_ref[1]) + mm_nt(d_v, w_ref[2]) + mm_nt(d_zb, w_ref[3])
    cot = cot.astype(BF).astype(F32)
    hat1 = hat1_ref[...]
    d_gain1 = jnp.sum(cot * hat1, axis=0, keepdims=True)
    d_bias1 = jnp.sum(cot, axis=0, keepdims=True)
    d_x = (upd + normal_back(cot * aff_ref[0:1, :], hat1, rs1_ref[...])).astype(BF)
    dx_ref[...] = mm_tn(turn, d_x).astype(BF)
    vectors = jnp.concatenate(
        [d_gain1, d_bias1, d_gate_bias, d_gain2, d_bias2, jnp.zeros((3, width), F32)], axis=0
    )
    grad_scr[base : base + 16, :] = jnp.concatenate([vectors[:, :128], vectors[:, 128:]], axis=0).astype(BF)
    base = base + 16
    grad_scr[base:, :] = jnp.zeros((grad_scr.shape[0] - base, 128), BF)
    half = keep_ref.shape[0]
    keep_ref[...] = grad_scr[pl.ds(pl.multiple_of(core * half, half), half), :]
    send_ref[...] = grad_scr[pl.ds(pl.multiple_of((1 - core) * half, half), half), :]


def unpack_kernel(where_ref, mine_ref, other_ref, att_ref, vec_ref, lrt_ref, final_ref, scr):
    core = where_ref[1]
    half = mine_ref.shape[0]
    scr[pl.ds(pl.multiple_of(core * half, half), half), :] = mine_ref[...]
    scr[pl.ds(pl.multiple_of((1 - core) * half, half), half), :] = other_ref[...]
    total = att_ref.shape[1]
    for w in range(5):
        for h in range(2):
            at = (2 * w + h) * total
            att_ref[w, :, h * 128 : (h + 1) * 128] = scr[at : at + total, :].astype(F32)
    base = 10 * total
    final_ref[...] = scr[base : base + 1024, :].astype(F32)
    base = base + 1024
    lrt_ref[:, :128] = scr[base : base + 64, :].astype(F32)
    lrt_ref[:, 128:] = scr[base + 64 : base + 128, :].astype(F32)
    base = base + 128
    vectors = scr[base : base + 16, :].astype(F32)
    vec_ref[:, :128] = vectors[:5]
    vec_ref[:, 128:] = vectors[8:13]


def call(kernel, outs, scratch, where, *args):
    vmem = pl.BlockSpec(memory_space=pltpu.VMEM)
    return pl.pallas_call(
        kernel,
        out_shape=[jax.ShapeDtypeStruct(s, d) for s, d in outs],
        in_specs=[pl.BlockSpec(memory_space=pltpu.SMEM)] + [vmem] * len(args),
        out_specs=[vmem] * len(outs),
        scratch_shapes=scratch,
        compiler_params=pltpu.CompilerParams(vmem_limit_bytes=48 * 1024 * 1024),
    )(where, *args)


def exchange(value, axes, total, offset):
    return lax.ppermute(value, axes, [(i, i ^ offset) for i in range(total)])


def reduce_gradients(keep, send, index, dp_size, axial_size):
    axes = ("dp", "axial")
    if axial_size != 2 or dp_size != 16:
        summed = lax.psum((keep.astype(F32), send.astype(F32)), axes)
        return summed[0].astype(BF), summed[1].astype(BF)
    total = dp_size * axial_size
    half = keep.shape[0]
    mine = keep.astype(F32) + exchange(send, axes, total, 2).astype(F32)
    place = (index % 2) + 2 * ((index // 4) % 2)
    offsets = (1, 4, 5)
    quarter = half // 4
    own = lax.dynamic_slice_in_dim(mine, place * quarter, quarter)
    got = []
    for step, offset in zip((1, 2, 3), offsets):
        piece = lax.dynamic_slice_in_dim(mine, (place ^ step) * quarter, quarter)
        got.append(exchange(piece.astype(BF), axes, total, offset))
    own = own + got[0].astype(F32) + got[1].astype(F32) + got[2].astype(F32)
    own = own.astype(BF)
    level = [exchange(own, axes, total, offset).astype(F32) for offset in (8, 16, 24)]
    own = ((own.astype(F32) + level[0]) + (level[1] + level[2])).astype(BF)
    pieces = [own] + [exchange(own, axes, total, offset) for offset in offsets]
    stacked = jnp.stack(pieces)
    mine = jnp.concatenate([lax.dynamic_index_in_dim(stacked, place ^ k, keepdims=False) for k in range(4)], axis=0)
    return mine, exchange(mine, axes, total, 2)


def per_device(
    dp_size,
    axial_size,
    homolog_activations,
    homolog_adjoint,
    duplex_adjoint,
    homolog_exists_filter,
    amino_exists_filter,
    focus_matrices_tier,
    affine_parameters,
    left_right_matrices,
    outer_final_matrix,
):
    n = axial_size
    _, seqs, rows, width = homolog_activations.shape
    total = seqs * rows
    index = lax.axis_index(("dp", "axial"))
    own = lax.axis_index("axial")
    fast = axial_size == 2 and dp_size == 16
    core = (index // 2) % 2 if fast else jnp.zeros_like(index)
    where = jnp.stack([own, core])
    x = homolog_activations.reshape(total, width)
    adj = homolog_adjoint.reshape(total, width)
    dup = duplex_adjoint.reshape(-1, DUPLEX_FEATURES)
    lrt = left_right_matrices.T
    flat_b, flat_f, column = ((total, width), BF), ((total, width), F32), ((total, 1), F32)
    block = rows * rows
    proj, pairs, *saved = call(
        partial(forward_kernel, n=n),
        [
            ((2 * OUTER_FACTORS, total), BF), ((n * block, DUPLEX_FEATURES), BF),
            flat_b, flat_b, flat_b, flat_b, flat_f, flat_f, flat_f, flat_b, flat_f, column, flat_f, column, flat_b,
        ],
        [pltpu.VMEM(dup.shape, F32)],
        where, x, dup, homolog_exists_filter, amino_exists_filter, focus_matrices_tier, affine_parameters, lrt,
    )
    other_proj, other_pairs = [], []
    for m in range(1, n):
        perm = [(a, (a - m) % n) for a in range(n)]
        at = ((n - m) % n) * block
        message = jnp.concatenate(
            [proj.reshape(-1, DUPLEX_FEATURES), pairs[at : at + block]], axis=0
        )
        message = lax.ppermute(message, "axial", perm)
        other_proj.append(message[:-block].reshape(proj.shape))
        other_pairs.append(message[-block:])
    used = 10 * total + outer_final_matrix.shape[0] + 128 + 16
    half = -(-used // 128) * 64
    dx, keep, send = call(
        partial(backward_kernel, n=n),
        [flat_b, ((half, 128), BF), ((half, 128), BF)],
        [pltpu.VMEM((2 * half, 128), BF)],
        where, proj, pairs, jnp.stack(other_proj), jnp.concatenate(other_pairs, axis=0), outer_final_matrix, adj,
        homolog_exists_filter, amino_exists_filter, focus_matrices_tier, affine_parameters, lrt, *saved,
    )
    mine, other = reduce_gradients(keep, send, index, dp_size, axial_size)
    grad_att, grad_vec, grad_lrt, grad_final = call(
        unpack_kernel,
        [
            (focus_matrices_tier.shape, F32), (affine_parameters.shape, F32), (lrt.shape, F32),
            (outer_final_matrix.shape, F32),
        ],
        [pltpu.VMEM((2 * half, 128), BF)],
        where, mine, other,
    )
    return (dx.reshape(homolog_activations.shape), grad_att, grad_vec, grad_lrt.T, grad_final)


def solution(mesh):
    return jax.shard_map(
        partial(per_device, mesh.shape["dp"], mesh.shape["axial"]),
        mesh=mesh,
        in_specs=(
            P("dp", None, "axial", None),
            P("dp", None, "axial", None),
            P("dp", "axial", None, None),
            P("dp", None),
            P("dp", None),
            P(),
            P(),
            P(),
            P(),
        ),
        out_specs=(P("dp", None, "axial", None), P(), P(), P(), P()),
        check_vma=False,
    )
```

time: 221 us -> 64.4 us (0.29)
  waiting for transfers between devices: 92.4 us -> 26 us
  blocking collectives: 47.8 us -> 0 us
  matrix products: 28.2 us -> 0 us
  starting transfers between devices: 0.08 us -> 14.9 us
  between operations: 15.2 us -> 0.88 us
  local copies, waits for them, and re-layouts: 24.5 us -> 11.3 us
  other arithmetic: 12.4 us -> 0.41 us
  Pallas kernels: 0 us -> 10.5 us
    psum x1 -> x0, waiting for transfers between devices: 92.3 us -> none  [per_device(): lax.psum((focus_derivative, affine_derivative, factor_derivative, pair_we...]
    psum x1 -> x0, blocking collectives: 41.5 us -> none  [per_device(): lax.psum((focus_derivative, affine_derivative, factor_derivative, pair_we...]
    dot_general x29 -> x0, matrix products: 28.2 us -> none  [the longest x3 4.03 us: pair_block(): jnp.einsum('sic,sje->ijce', left_part, right_part, precision=lax.Precisio...]
    ppermute x0 -> x12, waiting for transfers between devices: none -> 26 us  [the longest x11 24 us: exchange(): return lax.ppermute(value, axes, [(i, i ^ offset) for i in range(total)])]
    ppermute x0 -> x12, starting transfers between devices: none -> 14.9 us  [the longest x11 11.8 us: exchange(): return lax.ppermute(value, axes, [(i, i ^ offset) for i in range(total)])]
    pallas_call x0 -> x3, Pallas kernels: none -> 10.5 us  [call(): pl.pallas_call(kernel, out_shape=[jax.ShapeDtypeStruct(s, d) for s, d in...]
    convert_element_type x5 -> x1, local copies, waits for them, and re-layouts: 6.61 us -> 0.06 us  [reduce_gradients(): got.append(exchange(piece.astype(BF), axes, total, offset))]
    all_gather x1 -> x0, blocking collectives: 6.33 us -> none  [per_device(): right_all = lax.all_gather(right_own, 'axial', axis=1, tiled=True)]
  transfers between devices with their start and end apart: 2 -> 12, of which waited for: 1 -> 10; matrix products, arithmetic and copies ran while one was open for 7% -> 0% of each run, Pallas kernels for 0% -> 0%
where the time goes in v2:
time: 64.4 us; the launch traced here: 64 us
  waiting for transfers between devices  26 us (40%)
  starting transfers between devices  14.9 us (23%)
  local copies, waits for them, and re-layouts  11.3 us (18%)
  Pallas kernels  10.5 us (16%)
  between operations  0.88 us (1%)
    ppermute x11, waiting for transfers between devices, exchange(): return lax.ppermute(value, axes, [(i, i ^ offset) for i in range(total)])  24 us
    ppermute x11, starting transfers between devices, exchange(): return lax.ppermute(value, axes, [(i, i ^ offset) for i in range(total)])  11.8 us
    unnamed x44, local copies, waits for them, and re-layouts  11.1 us
    pallas_call x3, Pallas kernels, call(): pl.pallas_call(kernel, out_shape=[jax.ShapeDtypeStruct(s, d) for s, d in...  10.5 us
    ppermute x1, starting transfers between devices, per_device(): message = lax.ppermute(message, 'axial', perm)  3.03 us
    ppermute x1, waiting for transfers between devices, per_device(): message = lax.ppermute(message, 'axial', perm)  2.07 us
  transfers between devices with their start and end apart: 12, of which 10 were waited for; matrix products, arithmetic and copies ran while one was open for 0% of the time, Pallas kernels for 0%

profile of v2, /device:TPU:0, one launch (start us, length us, event | category | flops | bytes accessed | tf_op | source)
XLA Modules:
  0.0 64.0 jit_solution(13416452512177954839)
XLA Ops:
  0.8 1.1 %copy-done = bf16[5,256,256]{2,1,0:T(8,128)(2,1)S(1)} copy-done((bf16[5,256,256]{2,1,0:T(8,128)(2,1)S(1)}, bf16[5,256,256]{2,1,0:T(8,128)(2,1)}, u32[]{:S(2)}) %copy-start) | copy-done | bytes 655384
  2.6 0.9 %copy-done.14 = bf16[1,32,8,256]{3,2,1,0:T(8,128)(2,1)S(1)} copy-done((bf16[1,32,8,256]{3,2,1,0:T(8,128)(2,1)S(1)}, bf16[1,32,8,256]{3,2,1,0:T(8,128)(2,1)}, u32[]{:S(2)}) %copy-start.14) | copy-done | bytes 131096
  4.2 0.8 %copy-done.17 = bf16[1,8,16,128]{3,2,1,0:T(8,128)(2,1)S(1)} copy-done((bf16[1,8,16,128]{3,2,1,0:T(8,128)(2,1)S(1)}, bf16[1,8,16,128]{3,2,1,0:T(8,128)(2,1)}, u32[]{:S(2)}) %copy-start.17) | copy-done | bytes 32792
  6.3 2.9 %shard_map.128 = (bf16[64,256]{1,0:T(8,128)(2,1)S(1)}, bf16[128,128]{1,0:T(8,128)(2,1)S(1)}, bf16[256,256]{1,0:T(8,128)(2,1)S(1)}, bf16[256,256]{1,0:T(8,128)(2,...) custom-call(s32[2]{0:T(128)S(1)} %pad_add_fusion.where_ref, ...), custom_call_target="tpu_custom_call" | custom-call | tf_op jit(solution)/shard_map/pallas_call | solution.py:359
  11.2 3.0 %collective-permute-start = (bf16[192,128]{1,0:T(8,128)(2,1)S(1)}, bf16[192,128]{1,0:T(8,128)(2,1)S(1)}, u32[]{:S(2)}, u32[]{:S(2)}) collective-permute-start(bf16[192,128]{1,0:T(8,128)(2,1)S(1)} %pad_maximum_fusion.2), channel_id=1, source_target_pairs={{0,1},{1,0},{2,3},{3,2},{4,5},{5,4},{6,7},{7,6},{8,9},{9,8},{10,11... | collective-permute-start | bytes 147464 | tf_op jit(solution)/shard_map/ppermute | solution.py:442
  14.2 2.1 %collective-permute-done = bf16[192,128]{1,0:T(8,128)(2,1)S(1)} collective-permute-done((bf16[192,128]{1,0:T(8,128)(2,1)S(1)}, bf16[192,128]{1,0:T(8,128)(2,1)S(1)}, u32[]{:S(2)}, u32[]{:S(2)}) %collective-permute-start) | collective-permute-done | bytes 49184 | tf_op jit(solution)/shard_map/ppermute | solution.py:442
  16.4 0.9 %copy-done.7 = bf16[256,256]{1,0:T(8,128)(2,1)S(1)} copy-done((bf16[256,256]{1,0:T(8,128)(2,1)S(1)}, bf16[256,256]{1,0:T(8,128)(2,1)}, u32[]{:S(2)}) %copy-start.7) | copy-done | bytes 131096
  17.3 0.9 %copy-done.9 = f32[256,1]{1,0:T(8,128)S(1)} copy-done((f32[256,1]{1,0:T(8,128)S(1)}, f32[256,1]{1,0:T(8,128)}, u32[]{:S(2)}) %copy-start.9) | copy-done | bytes 1048
  18.2 0.9 %copy-done.11 = f32[256,1]{1,0:T(8,128)S(1)} copy-done((f32[256,1]{1,0:T(8,128)S(1)}, f32[256,1]{1,0:T(8,128)}, u32[]{:S(2)}) %copy-start.11) | copy-done | bytes 1048
  19.1 0.9 %copy-done.13 = bf16[256,256]{1,0:T(8,128)(2,1)S(1)} copy-done((bf16[256,256]{1,0:T(8,128)(2,1)S(1)}, bf16[256,256]{1,0:T(8,128)(2,1)}, u32[]{:S(2)}) %copy-start.13) | copy-done | bytes 131096
  20.0 5.7 %shard_map.129 = (bf16[256,256]{1,0:T(8,128)(2,1)}, bf16[1920,128]{1,0:T(8,128)(2,1)S(1)}, bf16[1920,128]{1,0:T(8,128)(2,1)}) custom-call(s32[2]{0:T(128)S(1)} %pad_add_fusion.where_ref, bf16[64,256]{1,0:T(8,128)(2,1)S(1)} %get-tuple-element.27.proj_ref, bf16[128,128]{1,0:T(8,128)(2,1)S(1)} %get-tuple-element.28.pairs_ref, ...), custom_call_target="tpu_custom_call" | custom-call | tf_op jit(solution)/shard_map/pallas_call | solution.py:359
  25.7 2.1 %collective-permute-done.1 = bf16[1920,128]{1,0:T(8,128)(2,1)S(1)} collective-permute-done((bf16[1920,128]{1,0:T(8,128)(2,1)}, bf16[1920,128]{1,0:T(8,128)(2,1)S(1)}, u32[]{:S(2)}, u32[]{:S(2)}) %collective-permute-start.1) | collective-permute-done | bytes 491552 | tf_op jit(solution)/shard_map/ppermute | solution.py:370
  28.0 3.0 %collective-permute-start.4 = (bf16[480,128]{1,0:T(8,128)(2,1)S(1)}, bf16[480,128]{1,0:T(8,128)(2,1)S(1)}, u32[]{:S(2)}, u32[]{:S(2)}) collective-permute-start(bf16[480,128]{1,0:T(8,128)(2,1)S(1)} %get-tuple-element.50), channel_id=1, source_target_pairs={{0,5},{1,4},{2,7},{3,6},{4,1},{5,0},{6,3},{7,2},{8,13},{9,12},{10,... | collective-permute-start | bytes 368648 | tf_op jit(solution)/shard_map/ppermute | solution.py:370
  31.6 3.5 %collective-permute-done.4 = bf16[480,128]{1,0:T(8,128)(2,1)S(1)} collective-permute-done((bf16[480,128]{1,0:T(8,128)(2,1)S(1)}, bf16[480,128]{1,0:T(8,128)(2,1)S(1)}, u32[]{:S(2)}, u32[]{:S(2)}) %collective-permute-start.4) | collective-permute-done | bytes 122912 | tf_op jit(solution)/shard_map/ppermute | solution.py:370
  35.1 2.4 %collective-permute-done.3 = bf16[480,128]{1,0:T(8,128)(2,1)S(1)} collective-permute-done((bf16[480,128]{1,0:T(8,128)(2,1)S(1)}, bf16[480,128]{1,0:T(8,128)(2,1)S(1)}, u32[]{:S(2)}, u32[]{:S(2)}) %collective-permute-start.3) | collective-permute-done | bytes 122912 | tf_op jit(solution)/shard_map/ppermute | solution.py:370
  37.6 3.7 %collective-permute-start.7 = (bf16[480,128]{1,0:T(8,128)(2,1)S(1)}, bf16[480,128]{1,0:T(8,128)(2,1)S(1)}, u32[]{:S(2)}, u32[]{:S(2)}) collective-permute-start(bf16[480,128]{1,0:T(8,128)(2,1)S(1)} %add_convert_fusion.1), channel_id=1, source_target_pairs={{0,24},{1,25},{2,26},{3,27},{4,28},{5,29},{6,30},{7,31},{8,16},{9,... | collective-permute-start | bytes 368648 | tf_op jit(solution)/shard_map/ppermute | solution.py:370
  41.2 0.8 %collective-permute-start.5 = (bf16[480,128]{1,0:T(8,128)(2,1)S(1)}, bf16[480,128]{1,0:T(8,128)(2,1)S(1)}, u32[]{:S(2)}, u32[]{:S(2)}) collective-permute-start(bf16[480,128]{1,0:T(8,128)(2,1)S(1)} %add_convert_fusion.1), channel_id=1, source_target_pairs={{0,8},{1,9},{2,10},{3,11},{4,12},{5,13},{6,14},{7,15},{8,0},{9,1},... | collective-permute-start | bytes 368648 | tf_op jit(solution)/shard_map/ppermute | solution.py:370
  42.0 3.7 %collective-permute-done.7 = bf16[480,128]{1,0:T(8,128)(2,1)S(1)} collective-permute-done((bf16[480,128]{1,0:T(8,128)(2,1)S(1)}, bf16[480,128]{1,0:T(8,128)(2,1)S(1)}, u32[]{:S(2)}, u32[]{:S(2)}) %collective-permute-start.7) | collective-permute-done | bytes 122912 | tf_op jit(solution)/shard_map/ppermute | solution.py:370
  45.7 5.5 %collective-permute-done.6 = bf16[480,128]{1,0:T(8,128)(2,1)S(1)} collective-permute-done((bf16[480,128]{1,0:T(8,128)(2,1)S(1)}, bf16[480,128]{1,0:T(8,128)(2,1)S(1)}, u32[]{:S(2)}, u32[]{:S(2)}) %collective-permute-start.6) | collective-permute-done | bytes 122912 | tf_op jit(solution)/shard_map/ppermute | solution.py:370
  51.3 3.0 %collective-permute-start.10 = (bf16[480,128]{1,0:T(8,128)(2,1)S(1)}, bf16[480,128]{1,0:T(8,128)(2,1)S(1)}, u32[]{:S(2)}, u32[]{:S(2)}) collective-permute-start(bf16[480,128]{1,0:T(8,128)(2,1)S(1)} %add_convert_fusion), channel_id=1, source_target_pairs={{0,5},{1,4},{2,7},{3,6},{4,1},{5,0},{6,3},{7,2},{8,13},{9,12},{10,... | collective-permute-start | bytes 368648 | tf_op jit(solution)/shard_map/ppermute | solution.py:370
  54.9 3.4 %collective-permute-done.10 = bf16[480,128]{1,0:T(8,128)(2,1)S(1)} collective-permute-done((bf16[480,128]{1,0:T(8,128)(2,1)S(1)}, bf16[480,128]{1,0:T(8,128)(2,1)S(1)}, u32[]{:S(2)}, u32[]{:S(2)}) %collective-permute-start.10) | collective-permute-done | bytes 122912 | tf_op jit(solution)/shard_map/ppermute | solution.py:370
  58.4 1.5 %collective-permute-done.9 = bf16[480,128]{1,0:T(8,128)(2,1)S(1)} collective-permute-done((bf16[480,128]{1,0:T(8,128)(2,1)S(1)}, bf16[480,128]{1,0:T(8,128)(2,1)S(1)}, u32[]{:S(2)}, u32[]{:S(2)}) %collective-permute-start.9) | collective-permute-done | bytes 122912 | tf_op jit(solution)/shard_map/ppermute | solution.py:370
  60.2 1.9 %collective-permute-done.11.other_ref = bf16[1920,128]{1,0:T(8,128)(2,1)S(1)} collective-permute-done((bf16[1920,128]{1,0:T(8,128)(2,1)S(1)}, bf16[1920,128]{1,0:T(8,128)(2,1)S(1)}, u32[]{:S(2)}, u32[]{:S(2)}) %collective-permute-start.11) | collective-permute-done | bytes 491552 | tf_op jit(solution)/shard_map/ppermute | solution.py:370
  62.0 1.9 %shard_map.130 = (f32[5,256,256]{2,1,0:T(8,128)}, f32[5,256]{1,0:T(8,128)}, f32[64,256]{1,0:T(8,128)}, f32[1024,128]{1,0:T(8,128)}) custom-call(s32[2]{0:T(128)S(1)} %pad_add_fusion.where_ref, bf16[1920,128]{1,0:T(8,128)(2,1)S(1)} %pad_maximum_fusion.1.mine_ref, bf16[1920,128]{1,0:T(8,128)(2,1)S(1)} %collective-permute-done.11.other_ref), custom_call_target="tpu_custom_call" | custom-call | tf_op jit(solution)/shard_map/pallas_call | solution.py:359
  (61 shorter events, 6.8 us)
Async XLA Ops:
  0.6 15.7 %copy-start.19 = (s32[1,32]{1,0:T(1,128)S(1)}, s32[1,32]{1,0:T(1,128)}, u32[]{:S(2)}) copy-start(s32[1,32]{1,0:T(1,128)} %seq_ref.3) | copy-start | bytes 388
  0.6 15.7 %copy-start.21 = (s32[1,16]{1,0:T(1,128)S(1)}, s32[1,16]{1,0:T(1,128)}, u32[]{:S(2)}) copy-start(s32[1,16]{1,0:T(1,128)} %res_ref.3) | copy-start | bytes 196
  0.7 15.7 %copy-start.16 = (f32[5,256]{1,0:T(8,128)S(1)}, f32[5,256]{1,0:T(8,128)}, u32[]{:S(2)}) copy-start(f32[5,256]{1,0:T(8,128)} %aff_ref.3) | copy-start | bytes 15364
  0.7 15.7 %copy-start.4 = (bf16[256,64]{0,1:T(8,128)(2,1)S(1)}, bf16[256,64]{0,1:T(8,128)(2,1)}, u32[]{:S(2)}) copy-start(bf16[256,64]{0,1:T(8,128)(2,1)} %param.16) | copy-start | bytes 98308
  0.8 1.1 %copy-start = (bf16[5,256,256]{2,1,0:T(8,128)(2,1)S(1)}, bf16[5,256,256]{2,1,0:T(8,128)(2,1)}, u32[]{:S(2)}) copy-start(bf16[5,256,256]{2,1,0:T(8,128)(2,1)} %w_ref.3) | copy-start | bytes 1966084
  2.6 0.9 %copy-start.14 = (bf16[1,32,8,256]{3,2,1,0:T(8,128)(2,1)S(1)}, bf16[1,32,8,256]{3,2,1,0:T(8,128)(2,1)}, u32[]{:S(2)}) copy-start(bf16[1,32,8,256]{3,2,1,0:T(8,128)(2,1)} %param.9) | copy-start | bytes 393220
  6.3 10.1 %copy-start.1 = (bf16[5,256,256]{2,1,0:T(8,128)(2,1)S(1)}, bf16[5,256,256]{2,1,0:T(8,128)(2,1)}, u32[]{:S(2)}) copy-start(bf16[5,256,256]{2,1,0:T(8,128)(2,1)} %w_ref.3) | copy-start | bytes 1966084
  6.3 10.1 %copy-start.2 = (bf16[1024,128]{1,0:T(8,128)(2,1)S(1)}, bf16[1024,128]{1,0:T(8,128)(2,1)}, u32[]{:S(2)}) copy-start(bf16[1024,128]{1,0:T(8,128)(2,1)} %wf_ref.1) | copy-start | bytes 786436
  6.3 10.1 %copy-start.5 = (bf16[1,32,8,256]{3,2,1,0:T(8,128)(2,1)S(1)}, bf16[1,32,8,256]{3,2,1,0:T(8,128)(2,1)}, u32[]{:S(2)}) copy-start(bf16[1,32,8,256]{3,2,1,0:T(8,128)(2,1)} %param.10) | copy-start | bytes 393220
  11.2 5.2 %copy-start.12 = (bf16[256,256]{1,0:T(8,128)(2,1)}, bf16[256,256]{1,0:T(8,128)(2,1)S(1)}, u32[]{:S(2)}) copy-start(bf16[256,256]{1,0:T(8,128)(2,1)S(1)} %get-tuple-element.41.sec_ref) | copy-start | bytes 393220
  11.2 5.1 %collective-permute-start = (bf16[192,128]{1,0:T(8,128)(2,1)S(1)}, bf16[192,128]{1,0:T(8,128)(2,1)S(1)}, u32[]{:S(2)}, u32[]{:S(2)}) collective-permute-start(bf16[192,128]{1,0:T(8,128)(2,1)S(1)} %pad_maximum_fusion.2), channel_id=1, source_target_pairs={{0,1},{1,0},{2,3},{3,2},{4,5},{5,4},{6,7},{7,6},{8,9},{9,8},{10,11... | collective-permute-start | bytes 147464 | tf_op jit(solution)/shard_map/ppermute | solution.py:442
  16.4 0.9 %copy-start.7 = (bf16[256,256]{1,0:T(8,128)(2,1)S(1)}, bf16[256,256]{1,0:T(8,128)(2,1)}, u32[]{:S(2)}) copy-start(bf16[256,256]{1,0:T(8,128)(2,1)} %copy-done.6) | copy-start | bytes 393220
  19.1 0.9 %copy-start.13 = (bf16[256,256]{1,0:T(8,128)(2,1)S(1)}, bf16[256,256]{1,0:T(8,128)(2,1)}, u32[]{:S(2)}) copy-start(bf16[256,256]{1,0:T(8,128)(2,1)} %copy-done.12) | copy-start | bytes 393220
  25.7 2.1 %collective-permute-start.1 = (bf16[1920,128]{1,0:T(8,128)(2,1)}, bf16[1920,128]{1,0:T(8,128)(2,1)S(1)}, u32[]{:S(2)}, u32[]{:S(2)}) collective-permute-start(bf16[1920,128]{1,0:T(8,128)(2,1)} %get-tuple-element.44), channel_id=1, source_target_pairs={{0,2},{1,3},{2,0},{3,1},{4,6},{5,7},{6,4},{7,5},{8,10},{9,11},{10,... | collective-permute-start | bytes 1474568 | tf_op jit(solution)/shard_map/ppermute | solution.py:370
  28.0 7.1 %collective-permute-start.4 = (bf16[480,128]{1,0:T(8,128)(2,1)S(1)}, bf16[480,128]{1,0:T(8,128)(2,1)S(1)}, u32[]{:S(2)}, u32[]{:S(2)}) collective-permute-start(bf16[480,128]{1,0:T(8,128)(2,1)S(1)} %get-tuple-element.50), channel_id=1, source_target_pairs={{0,5},{1,4},{2,7},{3,6},{4,1},{5,0},{6,3},{7,2},{8,13},{9,12},{10,... | collective-permute-start | bytes 368648 | tf_op jit(solution)/shard_map/ppermute | solution.py:370
  31.0 6.5 %collective-permute-start.3 = (bf16[480,128]{1,0:T(8,128)(2,1)S(1)}, bf16[480,128]{1,0:T(8,128)(2,1)S(1)}, u32[]{:S(2)}, u32[]{:S(2)}) collective-permute-start(bf16[480,128]{1,0:T(8,128)(2,1)S(1)} %get-tuple-element.51), channel_id=1, source_target_pairs={{0,4},{1,5},{2,6},{3,7},{4,0},{5,1},{6,2},{7,3},{8,12},{9,13},{10,... | collective-permute-start | bytes 368648 | tf_op jit(solution)/shard_map/ppermute | solution.py:370
  31.5 6.0 %collective-permute-start.2 = (bf16[480,128]{1,0:T(8,128)(2,1)S(1)}, bf16[480,128]{1,0:T(8,128)(2,1)S(1)}, u32[]{:S(2)}, u32[]{:S(2)}) collective-permute-start(bf16[480,128]{1,0:T(8,128)(2,1)S(1)} %get-tuple-element.49), channel_id=1, source_target_pairs={{0,1},{1,0},{2,3},{3,2},{4,5},{5,4},{6,7},{7,6},{8,9},{9,8},{10,11... | collective-permute-start | bytes 368648 | tf_op jit(solution)/shard_map/ppermute | solution.py:370
  37.6 8.2 %collective-permute-start.7 = (bf16[480,128]{1,0:T(8,128)(2,1)S(1)}, bf16[480,128]{1,0:T(8,128)(2,1)S(1)}, u32[]{:S(2)}, u32[]{:S(2)}) collective-permute-start(bf16[480,128]{1,0:T(8,128)(2,1)S(1)} %add_convert_fusion.1), channel_id=1, source_target_pairs={{0,24},{1,25},{2,26},{3,27},{4,28},{5,29},{6,30},{7,31},{8,16},{9,... | collective-permute-start | bytes 368648 | tf_op jit(solution)/shard_map/ppermute | solution.py:370
  41.2 10.0 %collective-permute-start.6 = (bf16[480,128]{1,0:T(8,128)(2,1)S(1)}, bf16[480,128]{1,0:T(8,128)(2,1)S(1)}, u32[]{:S(2)}, u32[]{:S(2)}) collective-permute-start(bf16[480,128]{1,0:T(8,128)(2,1)S(1)} %add_convert_fusion.1), channel_id=1, source_target_pairs={{0,16},{1,17},{2,18},{3,19},{4,20},{5,21},{6,22},{7,23},{8,24},{9,... | collective-permute-start | bytes 368648 | tf_op jit(solution)/shard_map/ppermute | solution.py:370
  41.2 10.0 %collective-permute-start.5 = (bf16[480,128]{1,0:T(8,128)(2,1)S(1)}, bf16[480,128]{1,0:T(8,128)(2,1)S(1)}, u32[]{:S(2)}, u32[]{:S(2)}) collective-permute-start(bf16[480,128]{1,0:T(8,128)(2,1)S(1)} %add_convert_fusion.1), channel_id=1, source_target_pairs={{0,8},{1,9},{2,10},{3,11},{4,12},{5,13},{6,14},{7,15},{8,0},{9,1},... | collective-permute-start | bytes 368648 | tf_op jit(solution)/shard_map/ppermute | solution.py:370
  51.3 7.1 %collective-permute-start.10 = (bf16[480,128]{1,0:T(8,128)(2,1)S(1)}, bf16[480,128]{1,0:T(8,128)(2,1)S(1)}, u32[]{:S(2)}, u32[]{:S(2)}) collective-permute-start(bf16[480,128]{1,0:T(8,128)(2,1)S(1)} %add_convert_fusion), channel_id=1, source_target_pairs={{0,5},{1,4},{2,7},{3,6},{4,1},{5,0},{6,3},{7,2},{8,13},{9,12},{10,... | collective-permute-start | bytes 368648 | tf_op jit(solution)/shard_map/ppermute | solution.py:370
  54.3 5.6 %collective-permute-start.9 = (bf16[480,128]{1,0:T(8,128)(2,1)S(1)}, bf16[480,128]{1,0:T(8,128)(2,1)S(1)}, u32[]{:S(2)}, u32[]{:S(2)}) collective-permute-start(bf16[480,128]{1,0:T(8,128)(2,1)S(1)} %add_convert_fusion), channel_id=1, source_target_pairs={{0,4},{1,5},{2,6},{3,7},{4,0},{5,1},{6,2},{7,3},{8,12},{9,13},{10,... | collective-permute-start | bytes 368648 | tf_op jit(solution)/shard_map/ppermute | solution.py:370
  54.8 5.1 %collective-permute-start.8 = (bf16[480,128]{1,0:T(8,128)(2,1)S(1)}, bf16[480,128]{1,0:T(8,128)(2,1)S(1)}, u32[]{:S(2)}, u32[]{:S(2)}) collective-permute-start(bf16[480,128]{1,0:T(8,128)(2,1)S(1)} %add_convert_fusion), channel_id=1, source_target_pairs={{0,1},{1,0},{2,3},{3,2},{4,5},{5,4},{6,7},{7,6},{8,9},{9,8},{10,11... | collective-permute-start | bytes 368648 | tf_op jit(solution)/shard_map/ppermute | solution.py:370
  60.1 1.9 %collective-permute-start.11 = (bf16[1920,128]{1,0:T(8,128)(2,1)S(1)}, bf16[1920,128]{1,0:T(8,128)(2,1)S(1)}, u32[]{:S(2)}, u32[]{:S(2)}) collective-permute-start(bf16[1920,128]{1,0:T(8,128)(2,1)S(1)} %pad_maximum_fusion.1.mine_ref), channel_id=1, source_target_pairs={{0,2},{1,3},{2,0},{3,1},{4,6},{5,7},{6,4},{7,5},{8,10},{9,11},{10,... | collective-permute-start | bytes 1474568 | tf_op jit(solution)/shard_map/ppermute | solution.py:370
  (10 other events, 7.3 us)

commit v3 on v2

--- a/solution.py
+++ b/solution.py
@@ -89,11 +89,22 @@
 
 
 def forward_kernel(
-    where_ref, x_ref, dup_ref, seq_ref, res_ref, w_ref, aff_ref, lrt_ref,
+    where_ref, x_hbm, dup_hbm, seq_hbm, res_hbm, w_hbm, aff_hbm, lrt_hbm, wf_hbm, adj_hbm,
     proj_ref, pairs_ref, nb_ref, q_ref, k_ref, v_ref, gate_ref, att_ref, p_ref, gated_ref,
-    hat1_ref, rs1_ref, hat2_ref, rs2_ref, sec_ref, dup_scr, *, n,
+    hat1_ref, rs1_ref, hat2_ref, rs2_ref, sec_ref, out_ref,
+    seq_ref, res_ref, w_ref, aff_ref, lrt_ref, wf_ref, adj_ref,
+    x_ref, dup_ref, dup_scr, sems, *, n,
 ):
     own = where_ref[0]
+    pairs_of = [
+        (x_hbm, x_ref), (aff_hbm, aff_ref), (seq_hbm, seq_ref), (res_hbm, res_ref), (dup_hbm, dup_ref),
+        (w_hbm, w_ref), (lrt_hbm, lrt_ref), (wf_hbm, wf_ref), (adj_hbm, adj_ref),
+    ]
+    copies = [pltpu.make_async_copy(src, dst, sems.at[i]) for i, (src, dst) in enumerate(pairs_of)]
+    for copy in copies:
+        copy.start()
+    for copy in copies[:5]:
+        copy.wait()
     seqs = seq_ref.shape[1]
     total = x_ref.shape[0]
     rows = total // seqs
@@ -115,13 +126,17 @@
     block = rows * rows
     for m in range(n):
         at = lax.rem(own + m, n) * block
-        pairs_ref[m * block : (m + 1) * block, :] = dup_scr[pl.ds(pl.multiple_of(at, block), block), :].astype(BF)
+        piece = dup_scr[pl.ds(pl.multiple_of(at, block), block), :].astype(BF)
+        pairs_ref[m * block : (m + 1) * block, :] = piece
+        if m > 0:
+            out_ref[n - 1 - m, 128:, :] = piece
     x = mm(to_residue_major(seqs, rows), x_ref[...])
     hat1, rs1 = normal_parts(x)
     hat1_ref[...] = hat1
     rs1_ref[...] = rs1
     nb = (hat1 * aff_ref[0:1, :] + aff_ref[1:2, :]).astype(BF)
     nb_ref[...] = nb
+    copies[5].wait()
     q = (mm(nb, w_ref[0]) * HEAD_DIM ** (-0.5)).astype(BF)
     k = mm(nb, w_ref[1]).astype(BF)
     v = mm(nb, w_ref[2]).astype(BF)
@@ -156,12 +171,18 @@
     rs2_ref[...] = rs2
     sec = (hat2 * aff_ref[3:4, :] + aff_ref[4:5, :]).astype(BF)
     sec_ref[...] = sec
+    for copy in copies[6:]:
+        copy.wait()
     proj = mm_nt(lrt_ref[...], sec)
     r, c = ids((sites, total))
     over_r = ones_where(r == c // seqs + own * rows)
     res8 = jnp.broadcast_to(res_f, (8, sites)).astype(BF)
     flags = seq_row * mm(res8, over_r)[0:1, :]
-    proj_ref[...] = (proj * flags).astype(BF)
+    proj = (proj * flags).astype(BF)
+    proj_ref[...] = proj
+    for m in range(n - 1):
+        out_ref[m, :64, :] = proj[:, :128]
+        out_ref[m, 64:128, :] = proj[:, 128:]
 
 
 def stack_right(right_t):
@@ -193,8 +214,55 @@
     return jnp.concatenate([d[g * 32 : (g + 1) * 32] for g in range(8)], axis=1)
 
 
+def sum_groups(value, seqs):
+    r, c = ids(value.shape)
+    kept = jnp.where(r // seqs == (c // 8) % 4, value, 0.0)
+    return jnp.sum(kept.reshape(4, seqs, value.shape[1]), axis=0)
+
+
+def outer_groups(outer, g):
+    o = outer[g * 32 : (g + 1) * 32]
+    return jnp.concatenate([o[:, b * 128 : (b + 1) * 128] for b in range(8)], axis=0)
+
+
+def widen(wf_ref):
+    return jnp.concatenate(
+        [
+            jnp.concatenate([wf_ref[g * 128 + b * 32 : g * 128 + (b + 1) * 32, :] for g in range(8)], axis=0)
+            for b in range(4)
+        ],
+        axis=1,
+    )
+
+
+def local_pairs_kernel(
+    proj_ref, pairs_ref, wf_ref, seq_ref, adj_ref,
+    cots_ref, left_ref, back_ref, right_cot_ref, final_ref, wide_ref, adj_out_ref, *, n,
+):
+    seqs = seq_ref.shape[1]
+    total = adj_ref.shape[0]
+    factors = OUTER_FACTORS
+    wide = widen(wf_ref)
+    wide_ref[...] = wide
+    both = proj_ref[...]
+    left = spread_left(both[:factors], seqs)
+    left_ref[...] = left
+    right = stack_right(both[factors:])
+    diags = [diagonal(pairs_ref[g * 32 : (g + 1) * 32, :]) for g in range(2 * n)]
+    cots = [pair_cotangent(wide, d) for d in diags]
+    for g in range(2 * n):
+        cots_ref[g * 32 : (g + 1) * 32, :] = cots[g]
+    near = jnp.concatenate(cots[:2], axis=0)
+    back_ref[...] = sum_groups(mm_tn(right, near), seqs)
+    right_cot_ref[...] = mm_nt(near, left)
+    outer = mm(right, left).astype(BF)
+    final_ref[...] = mm(outer_groups(outer, 0), diags[0]) + mm(outer_groups(outer, 1), diags[1])
+    adj_out_ref[...] = mm(to_residue_major(seqs, total // seqs), adj_ref[...])
+
+
 def backward_kernel(
-    where_ref, proj_ref, pairs_ref, other_proj_ref, other_pairs_ref, wf_ref, adj_ref, seq_ref, res_ref, w_ref, aff_ref,
+    where_ref, other_ref, pairs_ref, cots_ref, left_ref, back_ref, right_cot_ref, final_ref, wide_ref, adj_ref,
+    seq_ref, res_ref, w_ref, aff_ref,
     lrt_ref, nb_ref, q_ref, k_ref, v_ref, gate_ref, att_ref, p_ref, gated_ref, hat1_ref, rs1_ref,
     hat2_ref, rs2_ref, sec_ref,
     dx_ref, keep_ref, send_ref, grad_scr, *, n,
@@ -211,25 +279,16 @@
     res_f = res_ref[...].astype(F32)
     sites = res_ref.shape[1]
 
-    wide = jnp.concatenate(
-        [
-            jnp.concatenate([wf_ref[g * 128 + b * 32 : g * 128 + (b + 1) * 32, :] for g in range(8)], axis=0)
-            for b in range(4)
-        ],
-        axis=1,
-    )
-    rights, lefts = [], []
-    for m in range(n):
-        both = proj_ref[...] if m == 0 else other_proj_ref[m - 1]
-        lefts.append(spread_left(both[:factors], seqs))
+    wide = wide_ref[...]
+    rights = []
+    right_cot = right_cot_ref[...]
+    for m in range(1, n):
+        both = jnp.concatenate([other_ref[m - 1, :64, :], other_ref[m - 1, 64:128, :]], axis=1)
         rights.append(stack_right(both[factors:]))
+        inward = [pair_cotangent(wide, diagonal(other_ref[m - 1, 128 + g * 32 : 160 + g * 32, :])) for g in range(2)]
+        right_cot = right_cot + mm_nt(jnp.concatenate(inward, axis=0), spread_left(both[:factors], seqs))
     right = jnp.concatenate(rights, axis=0)
-    diags = [diagonal(pairs_ref[g * 32 : (g + 1) * 32, :]) for g in range(2 * n)]
-    cots = [pair_cotangent(wide, d) for d in diags]
-    back = mm_tn(right, jnp.concatenate(cots, axis=0))
-    r, c = ids(back.shape)
-    back = jnp.where(r // seqs == (c // 8) % 4, back, 0.0)
-    back = jnp.sum(back.reshape(4, seqs, back.shape[1]), axis=0)
+    back = back_ref[...] + sum_groups(mm_tn(right, cots_ref[block:, :]), seqs)
     tiles = []
     for g in range(8):
         t = back[:, g * 128 : (g + 1) * 128]
@@ -240,21 +299,12 @@
     back = jnp.where(c % 32 == 24 + r // seqs, jnp.concatenate([back] * rows, axis=0), jnp.zeros((), BF))
     r, c = ids((factors, back.shape[1]))
     left_cot = mm_nt(ones_where(c // 32 == r), back)
-    right_cot = mm_nt(jnp.concatenate(cots[:2], axis=0), lefts[0])
-    for m in range(1, n):
-        inward = [
-            pair_cotangent(wide, diagonal(other_pairs_ref[(m - 1) * block + g * 32 : (m - 1) * block + (g + 1) * 32, :]))
-            for g in range(2)
-        ]
-        right_cot = right_cot + mm_nt(jnp.concatenate(inward, axis=0), lefts[m])
     right_cot = right_cot.astype(BF).astype(F32)
     right_cot = jnp.concatenate([right_cot[:factors], right_cot[factors:]], axis=1)
-    outer = mm(right, lefts[0]).astype(BF)
-    final = jnp.zeros((256, 512), F32)
-    for g in range(2 * n):
-        o = outer[g * 32 : (g + 1) * 32]
-        o = jnp.concatenate([o[:, b * 128 : (b + 1) * 128] for b in range(8)], axis=0)
-        final = final + mm(o, diags[g])
+    outer = mm(right, left_ref[...]).astype(BF)
+    final = final_ref[...]
+    for g in range(2 * (n - 1)):
+        final = final + mm(outer_groups(outer, g), diagonal(pairs_ref[block + g * 32 : block + (g + 1) * 32, :]))
     base = 10 * total
     for g in range(8):
         for b in range(4):
@@ -271,12 +321,11 @@
     grad_scr[base : base + 64, :] = lr_grad[:, :128]
     grad_scr[base + 64 : base + 128, :] = lr_grad[:, 128:]
     base = base + 128
-    turn = to_residue_major(seqs, rows)
     cot = mm_tn(proj_cot, lrt_ref[...]).astype(BF).astype(F32)
     hat2 = hat2_ref[...]
     d_gain2 = jnp.sum(cot * hat2, axis=0, keepdims=True)
     d_bias2 = jnp.sum(cot, axis=0, keepdims=True)
-    upd = mm(turn, adj_ref[...]) + normal_back(cot * aff_ref[3:4, :], hat2, rs2_ref[...])
+    upd = adj_ref[...] + normal_back(cot * aff_ref[3:4, :], hat2, rs2_ref[...])
 
     def put(index, grad):
         grad = grad.astype(BF)
@@ -321,7 +370,7 @@
     d_gain1 = jnp.sum(cot * hat1, axis=0, keepdims=True)
     d_bias1 = jnp.sum(cot, axis=0, keepdims=True)
     d_x = (upd + normal_back(cot * aff_ref[0:1, :], hat1, rs1_ref[...])).astype(BF)
-    dx_ref[...] = mm_tn(turn, d_x).astype(BF)
+    dx_ref[...] = mm_tn(to_residue_major(seqs, rows), d_x).astype(BF)
     vectors = jnp.concatenate(
         [d_gain1, d_bias1, d_gate_bias, d_gain2, d_bias2, jnp.zeros((3, width), F32)], axis=0
     )
@@ -354,16 +403,15 @@
     vec_ref[:, 128:] = vectors[8:13]
 
 
-def call(kernel, outs, scratch, where, *args):
-    vmem = pl.BlockSpec(memory_space=pltpu.VMEM)
+def call(kernel, outs, scratch, where, *args, space=pltpu.VMEM):
     return pl.pallas_call(
         kernel,
         out_shape=[jax.ShapeDtypeStruct(s, d) for s, d in outs],
-        in_specs=[pl.BlockSpec(memory_space=pltpu.SMEM)] + [vmem] * len(args),
-        out_specs=[vmem] * len(outs),
+        in_specs=[pl.BlockSpec(memory_space=pltpu.SMEM)] * len(where) + [pl.BlockSpec(memory_space=space)] * len(args),
+        out_specs=[pl.BlockSpec(memory_space=pltpu.VMEM)] * len(outs),
         scratch_shapes=scratch,
-        compiler_params=pltpu.CompilerParams(vmem_limit_bytes=48 * 1024 * 1024),
-    )(where, *args)
+        compiler_params=pltpu.CompilerParams(vmem_limit_bytes=24 * 1024 * 1024),
+    )(*where, *[pltpu.with_memory_space_constraint(a, space) for a in args] if space != pltpu.VMEM else args)
 
 
 def exchange(value, axes, total, offset):
@@ -416,40 +464,44 @@
     own = lax.axis_index("axial")
     fast = axial_size == 2 and dp_size == 16
     core = (index // 2) % 2 if fast else jnp.zeros_like(index)
-    where = jnp.stack([own, core])
+    where = [jnp.stack([own, core])]
     x = homolog_activations.reshape(total, width)
     adj = homolog_adjoint.reshape(total, width)
     dup = duplex_adjoint.reshape(-1, DUPLEX_FEATURES)
     lrt = left_right_matrices.T
     flat_b, flat_f, column = ((total, width), BF), ((total, width), F32), ((total, 1), F32)
     block = rows * rows
-    proj, pairs, *saved = call(
+    lanes = OUTER_FACTORS * 32
+    inputs = (homolog_exists_filter, amino_exists_filter, focus_matrices_tier, affine_parameters, lrt, outer_final_matrix)
+    results = call(
         partial(forward_kernel, n=n),
         [
             ((2 * OUTER_FACTORS, total), BF), ((n * block, DUPLEX_FEATURES), BF),
             flat_b, flat_b, flat_b, flat_b, flat_f, flat_f, flat_f, flat_b, flat_f, column, flat_f, column, flat_b,
+            ((n - 1, 128 + block, DUPLEX_FEATURES), BF),
+        ] + [(a.shape, a.dtype) for a in (*inputs, adj)],
+        [pltpu.VMEM(x.shape, BF), pltpu.VMEM(dup.shape, BF), pltpu.VMEM(dup.shape, F32), pltpu.SemaphoreType.DMA((9,))],
+        where, x, dup, *inputs, adj, space=pltpu.HBM,
+    )
+    proj, pairs, saved, messages = results[0], results[1], results[2:15], results[15]
+    seq, res, w, aff, lrt, wf, adj = results[16:]
+    others = [lax.ppermute(messages[m - 1], "axial", [(a, (a - m) % n) for a in range(n)]) for m in range(1, n)]
+    near = call(
+        partial(local_pairs_kernel, n=n),
+        [
+            ((n * block, lanes), BF), ((128, lanes), BF), ((seqs, lanes), F32), ((block, 128), F32), ((256, 512), F32),
+            ((256, 512), BF), flat_f,
         ],
-        [pltpu.VMEM(dup.shape, F32)],
-        where, x, dup, homolog_exists_filter, amino_exists_filter, focus_matrices_tier, affine_parameters, lrt,
-    )
-    other_proj, other_pairs = [], []
-    for m in range(1, n):
-        perm = [(a, (a - m) % n) for a in range(n)]
-        at = ((n - m) % n) * block
-        message = jnp.concatenate(
-            [proj.reshape(-1, DUPLEX_FEATURES), pairs[at : at + block]], axis=0
-        )
-        message = lax.ppermute(message, "axial", perm)
-        other_proj.append(message[:-block].reshape(proj.shape))
-        other_pairs.append(message[-block:])
+        [],
+        [], proj, pairs, wf, seq, adj,
+    )
     used = 10 * total + outer_final_matrix.shape[0] + 128 + 16
     half = -(-used // 128) * 64
     dx, keep, send = call(
         partial(backward_kernel, n=n),
         [flat_b, ((half, 128), BF), ((half, 128), BF)],
         [pltpu.VMEM((2 * half, 128), BF)],
-        where, proj, pairs, jnp.stack(other_proj), jnp.concatenate(other_pairs, axis=0), outer_final_matrix, adj,
-        homolog_exists_filter, amino_exists_filter, focus_matrices_tier, affine_parameters, lrt, *saved,
+        where, jnp.stack(others), pairs, *near, seq, res, w, aff, lrt, *saved,
     )
     mine, other = reduce_gradients(keep, send, index, dp_size, axial_size)
     grad_att, grad_vec, grad_lrt, grad_final = call(

time: 64.4 us -> 53 us (0.82)
  local copies, waits for them, and re-layouts: 11.3 us -> 0.11 us
  Pallas kernels: 10.5 us -> 12.1 us
  waiting for transfers between devices: 26 us -> 24.7 us
    unnamed x44 -> x0, local copies, waits for them, and re-layouts: 11.1 us -> none
    pallas_call x3 -> x4, Pallas kernels: 10.5 us -> 12.1 us  [call(): pl.pallas_call(kernel, out_shape=[jax.ShapeDtypeStruct(s, d) for s, d in...]
    ppermute x1, waiting for transfers between devices: 2.07 us -> 0.91 us  [per_device(): lax.ppermute(messages[m - 1], 'axial', [(a, (a - m) % n) for a in range(n)])]
  transfers between devices with their start and end apart: 12 -> 12, of which waited for: 10 -> 11; matrix products, arithmetic and copies ran while one was open for 0% -> 0% of each run, Pallas kernels for 0% -> 2%
where the time goes in v3:
time: 53 us; the launch traced here: 52.8 us
  waiting for transfers between devices  24.7 us (47%)
  starting transfers between devices  14.7 us (28%)
  Pallas kernels  12.1 us (23%)
  between operations  0.73 us (1%)
    ppermute x11, waiting for transfers between devices, exchange(): return lax.ppermute(value, axes, [(i, i ^ offset) for i in range(total)])  23.8 us
    pallas_call x4, Pallas kernels, call(): pl.pallas_call(kernel, out_shape=[jax.ShapeDtypeStruct(s, d) for s, d in...  12.1 us
    ppermute x11, starting transfers between devices, exchange(): return lax.ppermute(value, axes, [(i, i ^ offset) for i in range(total)])  11.7 us
    ppermute x1, starting transfers between devices, per_device(): lax.ppermute(messages[m - 1], 'axial', [(a, (a - m) % n) for a in range(n)])  3.03 us
  transfers between devices with their start and end apart: 12, of which 11 were waited for; matrix products, arithmetic and copies ran while one was open for 0% of the time, Pallas kernels for 2%

profile of v3, /device:TPU:0, one launch (start us, length us, event | category | flops | bytes accessed | tf_op | source)
XLA Modules:
  0.0 52.8 jit_solution(5678726017207225540)
XLA Ops:
  0.7 4.0 %shard_map.128 = (bf16[64,256]{1,0:T(8,128)(2,1)S(1)}, bf16[128,128]{1,0:T(8,128)(2,1)S(1)}, bf16[256,256]{1,0:T(8,128)(2,1)S(1)}, bf16[256,256]{1,0:T(8,128)(2,...) custom-call(s32[2]{0:T(128)S(1)} %pad_add_fusion.where_ref, ...), custom_call_target="tpu_custom_call" | custom-call | tf_op jit(solution)/shard_map/pallas_call | solution.py:407
  4.8 3.0 %collective-permute-start = (bf16[192,128]{1,0:T(8,128)(2,1)S(1)}, bf16[192,128]{1,0:T(8,128)(2,1)S(1)}, u32[]{:S(2)}, u32[]{:S(2)}) collective-permute-start(bf16[192,128]{1,0:T(8,128)(2,1)S(1)} %bitcast.23), channel_id=1, source_target_pairs={{0,1},{1,0},{2,3},{3,2},{4,5},{5,4},{6,7},{7,6},{8,9},{9,8},{10,11... | collective-permute-start | bytes 147464 | tf_op jit(solution)/shard_map/ppermute | solution.py:488
  7.8 1.2 %shard_map.129 = (bf16[128,1024]{1,0:T(8,128)(2,1)S(1)}, bf16[128,1024]{1,0:T(8,128)(2,1)S(1)}, f32[32,1024]{1,0:T(8,128)S(1)}, f32[64,128]{1,0:T(8,128)S(1)}, f...) custom-call(bf16[64,256]{1,0:T(8,128)(2,1)S(1)} %get-tuple-element.44.proj_ref, ...), custom_call_target="tpu_custom_call" | custom-call | tf_op jit(solution)/shard_map/pallas_call | solution.py:407
  9.0 0.9 %collective-permute-done = bf16[192,128]{1,0:T(8,128)(2,1)S(1)} collective-permute-done((bf16[192,128]{1,0:T(8,128)(2,1)S(1)}, bf16[192,128]{1,0:T(8,128)(2,1)S(1)}, u32[]{:S(2)}, u32[]{:S(2)}) %collective-permute-start) | collective-permute-done | bytes 49184 | tf_op jit(solution)/shard_map/ppermute | solution.py:488
  9.9 5.0 %shard_map.130 = (bf16[256,256]{1,0:T(8,128)(2,1)}, bf16[1920,128]{1,0:T(8,128)(2,1)S(1)}, bf16[1920,128]{1,0:T(8,128)(2,1)S(1)}) custom-call(s32[2]{0:T(128)S(1)} %pad_add_fusion.where_ref, bf16[1,192,128]{2,1,0:T(8,128)(2,1)S(1)} %bitcast.22, bf16[128,128]{1,0:T(8,128)(2,1)S(1)} %get-tuple-element.43.pairs_ref, ...), custom_call_target="tpu_custom_call" | custom-call | tf_op jit(solution)/shard_map/pallas_call | solution.py:407
  14.9 1.9 %collective-permute-done.1 = bf16[1920,128]{1,0:T(8,128)(2,1)S(1)} collective-permute-done((bf16[1920,128]{1,0:T(8,128)(2,1)S(1)}, bf16[1920,128]{1,0:T(8,128)(2,1)S(1)}, u32[]{:S(2)}, u32[]{:S(2)}) %collective-permute-start.1) | collective-permute-done | bytes 491552 | tf_op jit(solution)/shard_map/ppermute | solution.py:418
  16.8 0.1 convert_add_fusion
  17.0 2.1 %collective-permute-start.2 = (bf16[480,128]{1,0:T(8,128)(2,1)S(1)}, bf16[480,128]{1,0:T(8,128)(2,1)S(1)}, u32[]{:S(2)}, u32[]{:S(2)}) collective-permute-start(bf16[480,128]{1,0:T(8,128)(2,1)S(1)} %get-tuple-element.79), channel_id=1, source_target_pairs={{0,1},{1,0},{2,3},{3,2},{4,5},{5,4},{6,7},{7,6},{8,9},{9,8},{10,11... | collective-permute-start | bytes 368648 | tf_op jit(solution)/shard_map/ppermute | solution.py:418
  19.0 1.5 %collective-permute-start.3 = (bf16[480,128]{1,0:T(8,128)(2,1)S(1)}, bf16[480,128]{1,0:T(8,128)(2,1)S(1)}, u32[]{:S(2)}, u32[]{:S(2)}) collective-permute-start(bf16[480,128]{1,0:T(8,128)(2,1)S(1)} %get-tuple-element.81), channel_id=1, source_target_pairs={{0,4},{1,5},{2,6},{3,7},{4,0},{5,1},{6,2},{7,3},{8,12},{9,13},{10,... | collective-permute-start | bytes 368648 | tf_op jit(solution)/shard_map/ppermute | solution.py:418
  20.6 2.1 %collective-permute-done.2 = bf16[480,128]{1,0:T(8,128)(2,1)S(1)} collective-permute-done((bf16[480,128]{1,0:T(8,128)(2,1)S(1)}, bf16[480,128]{1,0:T(8,128)(2,1)S(1)}, u32[]{:S(2)}, u32[]{:S(2)}) %collective-permute-start.2) | collective-permute-done | bytes 122912 | tf_op jit(solution)/shard_map/ppermute | solution.py:418
  22.7 2.6 %collective-permute-done.3 = bf16[480,128]{1,0:T(8,128)(2,1)S(1)} collective-permute-done((bf16[480,128]{1,0:T(8,128)(2,1)S(1)}, bf16[480,128]{1,0:T(8,128)(2,1)S(1)}, u32[]{:S(2)}, u32[]{:S(2)}) %collective-permute-start.3) | collective-permute-done | bytes 122912 | tf_op jit(solution)/shard_map/ppermute | solution.py:418
  25.3 1.3 %collective-permute-done.4 = bf16[480,128]{1,0:T(8,128)(2,1)S(1)} collective-permute-done((bf16[480,128]{1,0:T(8,128)(2,1)S(1)}, bf16[480,128]{1,0:T(8,128)(2,1)S(1)}, u32[]{:S(2)}, u32[]{:S(2)}) %collective-permute-start.4) | collective-permute-done | bytes 122912 | tf_op jit(solution)/shard_map/ppermute | solution.py:418
  26.6 1.8 %collective-permute-start.5 = (bf16[480,128]{1,0:T(8,128)(2,1)S(1)}, bf16[480,128]{1,0:T(8,128)(2,1)S(1)}, u32[]{:S(2)}, u32[]{:S(2)}) collective-permute-start(bf16[480,128]{1,0:T(8,128)(2,1)S(1)} %add_convert_fusion.1), channel_id=1, source_target_pairs={{0,8},{1,9},{2,10},{3,11},{4,12},{5,13},{6,14},{7,15},{8,0},{9,1},... | collective-permute-start | bytes 368648 | tf_op jit(solution)/shard_map/ppermute | solution.py:418
  28.4 2.6 %collective-permute-start.6 = (bf16[480,128]{1,0:T(8,128)(2,1)S(1)}, bf16[480,128]{1,0:T(8,128)(2,1)S(1)}, u32[]{:S(2)}, u32[]{:S(2)}) collective-permute-start(bf16[480,128]{1,0:T(8,128)(2,1)S(1)} %add_convert_fusion.1), channel_id=1, source_target_pairs={{0,16},{1,17},{2,18},{3,19},{4,20},{5,21},{6,22},{7,23},{8,24},{9,... | collective-permute-start | bytes 368648 | tf_op jit(solution)/shard_map/ppermute | solution.py:418
  31.1 1.8 %collective-permute-done.5 = bf16[480,128]{1,0:T(8,128)(2,1)S(1)} collective-permute-done((bf16[480,128]{1,0:T(8,128)(2,1)S(1)}, bf16[480,128]{1,0:T(8,128)(2,1)S(1)}, u32[]{:S(2)}, u32[]{:S(2)}) %collective-permute-start.5) | collective-permute-done | bytes 122912 | tf_op jit(solution)/shard_map/ppermute | solution.py:418
  32.9 7.2 %collective-permute-done.6 = bf16[480,128]{1,0:T(8,128)(2,1)S(1)} collective-permute-done((bf16[480,128]{1,0:T(8,128)(2,1)S(1)}, bf16[480,128]{1,0:T(8,128)(2,1)S(1)}, u32[]{:S(2)}, u32[]{:S(2)}) %collective-permute-start.6) | collective-permute-done | bytes 122912 | tf_op jit(solution)/shard_map/ppermute | solution.py:418
  40.1 1.4 %collective-permute-start.8 = (bf16[480,128]{1,0:T(8,128)(2,1)S(1)}, bf16[480,128]{1,0:T(8,128)(2,1)S(1)}, u32[]{:S(2)}, u32[]{:S(2)}) collective-permute-start(bf16[480,128]{1,0:T(8,128)(2,1)S(1)} %add_convert_fusion), channel_id=1, source_target_pairs={{0,1},{1,0},{2,3},{3,2},{4,5},{5,4},{6,7},{7,6},{8,9},{9,8},{10,11... | collective-permute-start | bytes 368648 | tf_op jit(solution)/shard_map/ppermute | solution.py:418
  41.5 1.5 %collective-permute-start.9 = (bf16[480,128]{1,0:T(8,128)(2,1)S(1)}, bf16[480,128]{1,0:T(8,128)(2,1)S(1)}, u32[]{:S(2)}, u32[]{:S(2)}) collective-permute-start(bf16[480,128]{1,0:T(8,128)(2,1)S(1)} %add_convert_fusion), channel_id=1, source_target_pairs={{0,4},{1,5},{2,6},{3,7},{4,0},{5,1},{6,2},{7,3},{8,12},{9,13},{10,... | collective-permute-start | bytes 368648 | tf_op jit(solution)/shard_map/ppermute | solution.py:418
  43.0 0.6 %collective-permute-start.10 = (bf16[480,128]{1,0:T(8,128)(2,1)S(1)}, bf16[480,128]{1,0:T(8,128)(2,1)S(1)}, u32[]{:S(2)}, u32[]{:S(2)}) collective-permute-start(bf16[480,128]{1,0:T(8,128)(2,1)S(1)} %add_convert_fusion), channel_id=1, source_target_pairs={{0,5},{1,4},{2,7},{3,6},{4,1},{5,0},{6,3},{7,2},{8,13},{9,12},{10,... | collective-permute-start | bytes 368648 | tf_op jit(solution)/shard_map/ppermute | solution.py:418
  43.6 1.4 %collective-permute-done.8 = bf16[480,128]{1,0:T(8,128)(2,1)S(1)} collective-permute-done((bf16[480,128]{1,0:T(8,128)(2,1)S(1)}, bf16[480,128]{1,0:T(8,128)(2,1)S(1)}, u32[]{:S(2)}, u32[]{:S(2)}) %collective-permute-start.8) | collective-permute-done | bytes 122912 | tf_op jit(solution)/shard_map/ppermute | solution.py:418
  45.0 1.4 %collective-permute-done.9 = bf16[480,128]{1,0:T(8,128)(2,1)S(1)} collective-permute-done((bf16[480,128]{1,0:T(8,128)(2,1)S(1)}, bf16[480,128]{1,0:T(8,128)(2,1)S(1)}, u32[]{:S(2)}, u32[]{:S(2)}) %collective-permute-start.9) | collective-permute-done | bytes 122912 | tf_op jit(solution)/shard_map/ppermute | solution.py:418
  46.4 2.4 %collective-permute-done.10 = bf16[480,128]{1,0:T(8,128)(2,1)S(1)} collective-permute-done((bf16[480,128]{1,0:T(8,128)(2,1)S(1)}, bf16[480,128]{1,0:T(8,128)(2,1)S(1)}, u32[]{:S(2)}, u32[]{:S(2)}) %collective-permute-start.10) | collective-permute-done | bytes 122912 | tf_op jit(solution)/shard_map/ppermute | solution.py:418
  49.1 1.9 %collective-permute-done.11.other_ref = bf16[1920,128]{1,0:T(8,128)(2,1)S(1)} collective-permute-done((bf16[1920,128]{1,0:T(8,128)(2,1)S(1)}, bf16[1920,128]{1,0:T(8,128)(2,1)S(1)}, u32[]{:S(2)}, u32[]{:S(2)}) %collective-permute-start.11) | collective-permute-done | bytes 491552 | tf_op jit(solution)/shard_map/ppermute | solution.py:418
  50.9 1.9 %shard_map.131 = (f32[5,256,256]{2,1,0:T(8,128)}, f32[5,256]{1,0:T(8,128)}, f32[64,256]{1,0:T(8,128)}, f32[1024,128]{1,0:T(8,128)}) custom-call(s32[2]{0:T(128)S(1)} %pad_add_fusion.where_ref, bf16[1920,128]{1,0:T(8,128)(2,1)S(1)} %pad_maximum_fusion.1.mine_ref, bf16[1920,128]{1,0:T(8,128)(2,1)S(1)} %collective-permute-done.11.other_ref), custom_call_target="tpu_custom_call" | custom-call | tf_op jit(solution)/shard_map/pallas_call | solution.py:407
  (12 shorter events, 0.6 us)
Async XLA Ops:
  4.8 5.1 %collective-permute-start = (bf16[192,128]{1,0:T(8,128)(2,1)S(1)}, bf16[192,128]{1,0:T(8,128)(2,1)S(1)}, u32[]{:S(2)}, u32[]{:S(2)}) collective-permute-start(bf16[192,128]{1,0:T(8,128)(2,1)S(1)} %bitcast.23), channel_id=1, source_target_pairs={{0,1},{1,0},{2,3},{3,2},{4,5},{5,4},{6,7},{7,6},{8,9},{9,8},{10,11... | collective-permute-start | bytes 147464 | tf_op jit(solution)/shard_map/ppermute | solution.py:488
  14.9 1.9 %collective-permute-start.1 = (bf16[1920,128]{1,0:T(8,128)(2,1)S(1)}, bf16[1920,128]{1,0:T(8,128)(2,1)S(1)}, u32[]{:S(2)}, u32[]{:S(2)}) collective-permute-start(bf16[1920,128]{1,0:T(8,128)(2,1)S(1)} %get-tuple-element.74), channel_id=1, source_target_pairs={{0,2},{1,3},{2,0},{3,1},{4,6},{5,7},{6,4},{7,5},{8,10},{9,11},{10,... | collective-permute-start | bytes 1474568 | tf_op jit(solution)/shard_map/ppermute | solution.py:418
  17.0 5.7 %collective-permute-start.2 = (bf16[480,128]{1,0:T(8,128)(2,1)S(1)}, bf16[480,128]{1,0:T(8,128)(2,1)S(1)}, u32[]{:S(2)}, u32[]{:S(2)}) collective-permute-start(bf16[480,128]{1,0:T(8,128)(2,1)S(1)} %get-tuple-element.79), channel_id=1, source_target_pairs={{0,1},{1,0},{2,3},{3,2},{4,5},{5,4},{6,7},{7,6},{8,9},{9,8},{10,11... | collective-permute-start | bytes 368648 | tf_op jit(solution)/shard_map/ppermute | solution.py:418
  19.0 6.2 %collective-permute-start.3 = (bf16[480,128]{1,0:T(8,128)(2,1)S(1)}, bf16[480,128]{1,0:T(8,128)(2,1)S(1)}, u32[]{:S(2)}, u32[]{:S(2)}) collective-permute-start(bf16[480,128]{1,0:T(8,128)(2,1)S(1)} %get-tuple-element.81), channel_id=1, source_target_pairs={{0,4},{1,5},{2,6},{3,7},{4,0},{5,1},{6,2},{7,3},{8,12},{9,13},{10,... | collective-permute-start | bytes 368648 | tf_op jit(solution)/shard_map/ppermute | solution.py:418
  20.5 6.0 %collective-permute-start.4 = (bf16[480,128]{1,0:T(8,128)(2,1)S(1)}, bf16[480,128]{1,0:T(8,128)(2,1)S(1)}, u32[]{:S(2)}, u32[]{:S(2)}) collective-permute-start(bf16[480,128]{1,0:T(8,128)(2,1)S(1)} %get-tuple-element.80), channel_id=1, source_target_pairs={{0,5},{1,4},{2,7},{3,6},{4,1},{5,0},{6,3},{7,2},{8,13},{9,12},{10,... | collective-permute-start | bytes 368648 | tf_op jit(solution)/shard_map/ppermute | solution.py:418
  26.6 6.2 %collective-permute-start.5 = (bf16[480,128]{1,0:T(8,128)(2,1)S(1)}, bf16[480,128]{1,0:T(8,128)(2,1)S(1)}, u32[]{:S(2)}, u32[]{:S(2)}) collective-permute-start(bf16[480,128]{1,0:T(8,128)(2,1)S(1)} %add_convert_fusion.1), channel_id=1, source_target_pairs={{0,8},{1,9},{2,10},{3,11},{4,12},{5,13},{6,14},{7,15},{8,0},{9,1},... | collective-permute-start | bytes 368648 | tf_op jit(solution)/shard_map/ppermute | solution.py:418
  28.4 11.6 %collective-permute-start.6 = (bf16[480,128]{1,0:T(8,128)(2,1)S(1)}, bf16[480,128]{1,0:T(8,128)(2,1)S(1)}, u32[]{:S(2)}, u32[]{:S(2)}) collective-permute-start(bf16[480,128]{1,0:T(8,128)(2,1)S(1)} %add_convert_fusion.1), channel_id=1, source_target_pairs={{0,16},{1,17},{2,18},{3,19},{4,20},{5,21},{6,22},{7,23},{8,24},{9,... | collective-permute-start | bytes 368648 | tf_op jit(solution)/shard_map/ppermute | solution.py:418
  31.0 9.0 %collective-permute-start.7 = (bf16[480,128]{1,0:T(8,128)(2,1)S(1)}, bf16[480,128]{1,0:T(8,128)(2,1)S(1)}, u32[]{:S(2)}, u32[]{:S(2)}) collective-permute-start(bf16[480,128]{1,0:T(8,128)(2,1)S(1)} %add_convert_fusion.1), channel_id=1, source_target_pairs={{0,24},{1,25},{2,26},{3,27},{4,28},{5,29},{6,30},{7,31},{8,16},{9,... | collective-permute-start | bytes 368648 | tf_op jit(solution)/shard_map/ppermute | solution.py:418
  40.1 5.0 %collective-permute-start.8 = (bf16[480,128]{1,0:T(8,128)(2,1)S(1)}, bf16[480,128]{1,0:T(8,128)(2,1)S(1)}, u32[]{:S(2)}, u32[]{:S(2)}) collective-permute-start(bf16[480,128]{1,0:T(8,128)(2,1)S(1)} %add_convert_fusion), channel_id=1, source_target_pairs={{0,1},{1,0},{2,3},{3,2},{4,5},{5,4},{6,7},{7,6},{8,9},{9,8},{10,11... | collective-permute-start | bytes 368648 | tf_op jit(solution)/shard_map/ppermute | solution.py:418
  41.5 4.9 %collective-permute-start.9 = (bf16[480,128]{1,0:T(8,128)(2,1)S(1)}, bf16[480,128]{1,0:T(8,128)(2,1)S(1)}, u32[]{:S(2)}, u32[]{:S(2)}) collective-permute-start(bf16[480,128]{1,0:T(8,128)(2,1)S(1)} %add_convert_fusion), channel_id=1, source_target_pairs={{0,4},{1,5},{2,6},{3,7},{4,0},{5,1},{6,2},{7,3},{8,12},{9,13},{10,... | collective-permute-start | bytes 368648 | tf_op jit(solution)/shard_map/ppermute | solution.py:418
  43.0 5.8 %collective-permute-start.10 = (bf16[480,128]{1,0:T(8,128)(2,1)S(1)}, bf16[480,128]{1,0:T(8,128)(2,1)S(1)}, u32[]{:S(2)}, u32[]{:S(2)}) collective-permute-start(bf16[480,128]{1,0:T(8,128)(2,1)S(1)} %add_convert_fusion), channel_id=1, source_target_pairs={{0,5},{1,4},{2,7},{3,6},{4,1},{5,0},{6,3},{7,2},{8,13},{9,12},{10,... | collective-permute-start | bytes 368648 | tf_op jit(solution)/shard_map/ppermute | solution.py:418
  49.0 1.9 %collective-permute-start.11 = (bf16[1920,128]{1,0:T(8,128)(2,1)S(1)}, bf16[1920,128]{1,0:T(8,128)(2,1)S(1)}, u32[]{:S(2)}, u32[]{:S(2)}) collective-permute-start(bf16[1920,128]{1,0:T(8,128)(2,1)S(1)} %pad_maximum_fusion.1.mine_ref), channel_id=1, source_target_pairs={{0,2},{1,3},{2,0},{3,1},{4,6},{5,7},{6,4},{7,5},{8,10},{9,11},{10,... | collective-permute-start | bytes 1474568 | tf_op jit(solution)/shard_map/ppermute | solution.py:418

commit v4 on v3

--- a/solution.py
+++ b/solution.py
@@ -260,25 +260,26 @@
     adj_out_ref[...] = mm(to_residue_major(seqs, total // seqs), adj_ref[...])
 
 
-def backward_kernel(
-    where_ref, other_ref, pairs_ref, cots_ref, left_ref, back_ref, right_cot_ref, final_ref, wide_ref, adj_ref,
-    seq_ref, res_ref, w_ref, aff_ref,
-    lrt_ref, nb_ref, q_ref, k_ref, v_ref, gate_ref, att_ref, p_ref, gated_ref, hat1_ref, rs1_ref,
-    hat2_ref, rs2_ref, sec_ref,
-    dx_ref, keep_ref, send_ref, grad_scr, *, n,
+def split_halves(core, keep_ref, send_ref, grad_scr):
+    half = keep_ref.shape[0]
+    keep_ref[...] = grad_scr[pl.ds(pl.multiple_of(core * half, half), half), :]
+    send_ref[...] = grad_scr[pl.ds(pl.multiple_of((1 - core) * half, half), half), :]
+
+
+def pairs_kernel(
+    where_ref, other_ref, pairs_ref, cots_ref, left_ref, back_ref, right_cot_ref, final_ref, wide_ref,
+    seq_ref, res_ref, sec_ref,
+    proj_cot_ref, keep_ref, send_ref, grad_scr, *, n,
 ):
     own, core = where_ref[0], where_ref[1]
     seqs = seq_ref.shape[1]
-    total, width = adj_ref.shape
+    total = sec_ref.shape[0]
     rows = total // seqs
     block = rows * rows
     factors = OUTER_FACTORS
-    mask = head_mask(width)
-    same = ones_where(mask)
     seq_f = seq_ref[...].astype(F32)
     res_f = res_ref[...].astype(F32)
     sites = res_ref.shape[1]
-
     wide = wide_ref[...]
     rights = []
     right_cot = right_cot_ref[...]
@@ -301,27 +302,37 @@
     left_cot = mm_nt(ones_where(c // 32 == r), back)
     right_cot = right_cot.astype(BF).astype(F32)
     right_cot = jnp.concatenate([right_cot[:factors], right_cot[factors:]], axis=1)
-    outer = mm(right, left_ref[...]).astype(BF)
-    final = final_ref[...]
-    for g in range(2 * (n - 1)):
-        final = final + mm(outer_groups(outer, g), diagonal(pairs_ref[block + g * 32 : block + (g + 1) * 32, :]))
-    base = 10 * total
-    for g in range(8):
-        for b in range(4):
-            at = base + (4 * g + b) * 32
-            grad_scr[at : at + 32, :] = final[g * 32 : (g + 1) * 32, b * 128 : (b + 1) * 128].astype(BF)
-
     r, c = ids((seqs, total))
     seq_row = mm(jnp.broadcast_to(seq_f, (8, seqs)).astype(BF), ones_where(r == c % seqs))[0:1, :]
     r, c = ids((sites, total))
     res_row = mm(jnp.broadcast_to(res_f, (8, sites)).astype(BF), ones_where(r == c // seqs + own * rows))[0:1, :]
     proj_cot = (jnp.concatenate([left_cot, right_cot], axis=0) * (seq_row * res_row)).astype(BF)
-    base = base + 1024
+    proj_cot_ref[...] = proj_cot
     lr_grad = mm(proj_cot, sec_ref[...]).astype(BF)
-    grad_scr[base : base + 64, :] = lr_grad[:, :128]
-    grad_scr[base + 64 : base + 128, :] = lr_grad[:, 128:]
-    base = base + 128
-    cot = mm_tn(proj_cot, lrt_ref[...]).astype(BF).astype(F32)
+    grad_scr[1024:1088, :] = lr_grad[:, :128]
+    grad_scr[1088:1152, :] = lr_grad[:, 128:]
+    outer = mm(right, left_ref[...]).astype(BF)
+    final = final_ref[...]
+    for g in range(2 * (n - 1)):
+        final = final + mm(outer_groups(outer, g), diagonal(pairs_ref[block + g * 32 : block + (g + 1) * 32, :]))
+    for g in range(8):
+        for b in range(4):
+            at = (4 * g + b) * 32
+            grad_scr[at : at + 32, :] = final[g * 32 : (g + 1) * 32, b * 128 : (b + 1) * 128].astype(BF)
+    split_halves(core, keep_ref, send_ref, grad_scr)
+
+
+def attention_kernel(
+    where_ref, proj_cot_ref, adj_ref, w_ref, aff_ref, lrt_ref, nb_ref, q_ref, k_ref, v_ref, gate_ref, att_ref, p_ref,
+    gated_ref, hat1_ref, rs1_ref, hat2_ref, rs2_ref,
+    dx_ref, keep_ref, send_ref, grad_scr, *, seqs,
+):
+    core = where_ref[1]
+    total, width = adj_ref.shape
+    rows = total // seqs
+    mask = head_mask(width)
+    same = ones_where(mask)
+    cot = mm_tn(proj_cot_ref[...], lrt_ref[...]).astype(BF).astype(F32)
     hat2 = hat2_ref[...]
     d_gain2 = jnp.sum(cot * hat2, axis=0, keepdims=True)
     d_bias2 = jnp.sum(cot, axis=0, keepdims=True)
@@ -374,30 +385,33 @@
     vectors = jnp.concatenate(
         [d_gain1, d_bias1, d_gate_bias, d_gain2, d_bias2, jnp.zeros((3, width), F32)], axis=0
     )
+    base = 10 * total
     grad_scr[base : base + 16, :] = jnp.concatenate([vectors[:, :128], vectors[:, 128:]], axis=0).astype(BF)
-    base = base + 16
-    grad_scr[base:, :] = jnp.zeros((grad_scr.shape[0] - base, 128), BF)
-    half = keep_ref.shape[0]
-    keep_ref[...] = grad_scr[pl.ds(pl.multiple_of(core * half, half), half), :]
-    send_ref[...] = grad_scr[pl.ds(pl.multiple_of((1 - core) * half, half), half), :]
-
-
-def unpack_kernel(where_ref, mine_ref, other_ref, att_ref, vec_ref, lrt_ref, final_ref, scr):
-    core = where_ref[1]
+    grad_scr[base + 16 :, :] = jnp.zeros((grad_scr.shape[0] - base - 16, 128), BF)
+    split_halves(core, keep_ref, send_ref, grad_scr)
+
+
+def join_halves(core, mine_ref, other_ref, scr):
     half = mine_ref.shape[0]
     scr[pl.ds(pl.multiple_of(core * half, half), half), :] = mine_ref[...]
     scr[pl.ds(pl.multiple_of((1 - core) * half, half), half), :] = other_ref[...]
+
+
+def unpack_pairs_kernel(where_ref, mine_ref, other_ref, lrt_ref, final_ref, scr):
+    join_halves(where_ref[1], mine_ref, other_ref, scr)
+    final_ref[...] = scr[:1024, :].astype(F32)
+    lrt_ref[:, :128] = scr[1024:1088, :].astype(F32)
+    lrt_ref[:, 128:] = scr[1088:1152, :].astype(F32)
+
+
+def unpack_attention_kernel(where_ref, mine_ref, other_ref, att_ref, vec_ref, scr):
+    join_halves(where_ref[1], mine_ref, other_ref, scr)
     total = att_ref.shape[1]
     for w in range(5):
         for h in range(2):
             at = (2 * w + h) * total
             att_ref[w, :, h * 128 : (h + 1) * 128] = scr[at : at + total, :].astype(F32)
     base = 10 * total
-    final_ref[...] = scr[base : base + 1024, :].astype(F32)
-    base = base + 1024
-    lrt_ref[:, :128] = scr[base : base + 64, :].astype(F32)
-    lrt_ref[:, 128:] = scr[base + 64 : base + 128, :].astype(F32)
-    base = base + 128
     vectors = scr[base : base + 16, :].astype(F32)
     vec_ref[:, :128] = vectors[:5]
     vec_ref[:, 128:] = vectors[8:13]
@@ -495,21 +509,32 @@
         [],
         [], proj, pairs, wf, seq, adj,
     )
-    used = 10 * total + outer_final_matrix.shape[0] + 128 + 16
-    half = -(-used // 128) * 64
+    *near, adj = near
+    half_pairs = (outer_final_matrix.shape[0] + 128) // 2
+    proj_cot, keep, send = call(
+        partial(pairs_kernel, n=n),
+        [(proj.shape, BF), ((half_pairs, 128), BF), ((half_pairs, 128), BF)],
+        [pltpu.VMEM((2 * half_pairs, 128), BF)],
+        where, jnp.stack(others), pairs, *near, seq, res, saved[-1],
+    )
+    mine, other = reduce_gradients(keep, send, index, dp_size, axial_size)
+    grad_lrt, grad_final = call(
+        unpack_pairs_kernel,
+        [(lrt.shape, F32), (outer_final_matrix.shape, F32)],
+        [pltpu.VMEM((2 * half_pairs, 128), BF)],
+        where, mine, other,
+    )
+    half = -(-(10 * total + 16) // 64) * 32
     dx, keep, send = call(
-        partial(backward_kernel, n=n),
+        partial(attention_kernel, seqs=seqs),
         [flat_b, ((half, 128), BF), ((half, 128), BF)],
         [pltpu.VMEM((2 * half, 128), BF)],
-        where, jnp.stack(others), pairs, *near, seq, res, w, aff, lrt, *saved,
+        where, proj_cot, adj, w, aff, lrt, *saved[:-1],
     )
     mine, other = reduce_gradients(keep, send, index, dp_size, axial_size)
-    grad_att, grad_vec, grad_lrt, grad_final = call(
-        unpack_kernel,
-        [
-            (focus_matrices_tier.shape, F32), (affine_parameters.shape, F32), (lrt.shape, F32),
-            (outer_final_matrix.shape, F32),
-        ],
+    grad_att, grad_vec = call(
+        unpack_attention_kernel,
+        [(focus_matrices_tier.shape, F32), (affine_parameters.shape, F32)],
         [pltpu.VMEM((2 * half, 128), BF)],
         where, mine, other,
     )

time: 53 us -> 54.3 us (1.025)
  waiting for transfers between devices: 24.7 us -> 10 us
  starting transfers between devices: 14.7 us -> 27.3 us
  Pallas kernels: 12.1 us -> 14.4 us
  other arithmetic: 0.44 us -> 1.35 us
    ppermute x11 -> x22, waiting for transfers between devices: 23.8 us -> 9.11 us  [exchange(): return lax.ppermute(value, axes, [(i, i ^ offset) for i in range(total)])]
    ppermute x11 -> x22, starting transfers between devices: 11.7 us -> 24.3 us  [exchange(): return lax.ppermute(value, axes, [(i, i ^ offset) for i in range(total)])]
    pallas_call x4 -> x6, Pallas kernels: 12.1 us -> 14.4 us  [call(): pl.pallas_call(kernel, out_shape=[jax.ShapeDtypeStruct(s, d) for s, d in...]
    add x1 -> x2, other arithmetic: 0.13 us -> 1.03 us  [reduce_gradients(): mine = keep.astype(F32) + exchange(send, axes, total, 2).astype(F32)]
  transfers between devices with their start and end apart: 12 -> 23, of which waited for: 11 -> 8; matrix products, arithmetic and copies ran while one was open for 0% -> 2% of each run, Pallas kernels for 2% -> 11%
where the time goes in v4:
time: 54.3 us; the launch traced here: 54.1 us
  starting transfers between devices  27.3 us (50%)
  Pallas kernels  14.4 us (27%)
  waiting for transfers between devices  10 us (18%)
  other arithmetic  1.35 us (2%)
  between operations  0.89 us (2%)
    ppermute x22, starting transfers between devices, exchange(): return lax.ppermute(value, axes, [(i, i ^ offset) for i in range(total)])  24.3 us
    pallas_call x6, Pallas kernels, call(): pl.pallas_call(kernel, out_shape=[jax.ShapeDtypeStruct(s, d) for s, d in...  14.4 us
    ppermute x22, waiting for transfers between devices, exchange(): return lax.ppermute(value, axes, [(i, i ^ offset) for i in range(total)])  9.11 us
    ppermute x1, starting transfers between devices, per_device(): lax.ppermute(messages[m - 1], 'axial', [(a, (a - m) % n) for a in range(n)])  3.03 us
  transfers between devices with their start and end apart: 23, of which 8 were waited for; matrix products, arithmetic and copies ran while one was open for 2% of the time, Pallas kernels for 11%

profile of v4, /device:TPU:0, one launch (start us, length us, event | category | flops | bytes accessed | tf_op | source)
XLA Modules:
  0.0 54.1 jit_solution(588720410304440758)
XLA Ops:
  0.7 4.0 %shard_map.128 = (bf16[64,256]{1,0:T(8,128)(2,1)S(1)}, bf16[128,128]{1,0:T(8,128)(2,1)S(1)}, bf16[256,256]{1,0:T(8,128)(2,1)S(1)}, bf16[256,256]{1,0:T(8,128)(2,...) custom-call(s32[2]{0:T(128)S(1)} %pad_add_fusion.where_ref, ...), custom_call_target="tpu_custom_call" | custom-call | tf_op jit(solution)/shard_map/pallas_call | solution.py:421
  4.8 3.0 %collective-permute-start = (bf16[192,128]{1,0:T(8,128)(2,1)S(1)}, bf16[192,128]{1,0:T(8,128)(2,1)S(1)}, u32[]{:S(2)}, u32[]{:S(2)}) collective-permute-start(bf16[192,128]{1,0:T(8,128)(2,1)S(1)} %bitcast.35), channel_id=1, source_target_pairs={{0,1},{1,0},{2,3},{3,2},{4,5},{5,4},{6,7},{7,6},{8,9},{9,8},{10,11... | collective-permute-start | bytes 147464 | tf_op jit(solution)/shard_map/ppermute | solution.py:502
  7.8 1.2 %shard_map.129 = (bf16[128,1024]{1,0:T(8,128)(2,1)S(1)}, bf16[128,1024]{1,0:T(8,128)(2,1)S(1)}, f32[32,1024]{1,0:T(8,128)S(1)}, f32[64,128]{1,0:T(8,128)S(1)}, f...) custom-call(bf16[64,256]{1,0:T(8,128)(2,1)S(1)} %get-tuple-element.47.proj_ref, ...), custom_call_target="tpu_custom_call" | custom-call | tf_op jit(solution)/shard_map/pallas_call | solution.py:421
  9.9 2.5 %shard_map.130 = (bf16[64,256]{1,0:T(8,128)(2,1)S(1)}, bf16[576,128]{1,0:T(8,128)(2,1)S(1)}, bf16[576,128]{1,0:T(8,128)(2,1)S(1)}) custom-call(s32[2]{0:T(128)S(1)} %pad_add_fusion.where_ref, bf16[1,192,128]{2,1,0:T(8,128)(2,1)S(1)} %bitcast.34, bf16[128,128]{1,0:T(8,128)(2,1)S(1)} %get-tuple-element.46.pairs_ref, ...), custom_call_target="tpu_custom_call" | custom-call | tf_op jit(solution)/shard_map/pallas_call | solution.py:421
  12.6 3.6 %shard_map.131 = (bf16[256,256]{1,0:T(8,128)(2,1)}, bf16[1312,128]{1,0:T(8,128)(2,1)S(1)}, bf16[1312,128]{1,0:T(8,128)(2,1)S(1)}) custom-call(s32[2]{0:T(128)S(1)} %pad_add_fusion.where_ref, bf16[64,256]{1,0:T(8,128)(2,1)S(1)} %get-tuple-element.59.proj_cot_ref, f32[256,256]{1,0:T(8,128)S(1)} %get-tuple-element.60.adj_ref, ...), custom_call_target="tpu_custom_call" | custom-call | tf_op jit(solution)/shard_map/pallas_call | solution.py:421
  17.5 2.1 %collective-permute-start.13 = (bf16[144,128]{1,0:T(8,128)(2,1)S(1)}, bf16[144,128]{1,0:T(8,128)(2,1)S(1)}, u32[]{:S(2)}, u32[]{:S(2)}) collective-permute-start(bf16[144,128]{1,0:T(8,128)(2,1)S(1)} %get-tuple-element.92), channel_id=1, source_target_pairs={{0,1},{1,0},{2,3},{3,2},{4,5},{5,4},{6,7},{7,6},{8,9},{9,8},{10,11... | collective-permute-start | bytes 110600 | tf_op jit(solution)/shard_map/ppermute | solution.py:432
  19.6 1.5 %collective-permute-start.14 = (bf16[144,128]{1,0:T(8,128)(2,1)S(1)}, bf16[144,128]{1,0:T(8,128)(2,1)S(1)}, u32[]{:S(2)}, u32[]{:S(2)}) collective-permute-start(bf16[144,128]{1,0:T(8,128)(2,1)S(1)} %get-tuple-element.94), channel_id=1, source_target_pairs={{0,4},{1,5},{2,6},{3,7},{4,0},{5,1},{6,2},{7,3},{8,12},{9,13},{10,... | collective-permute-start | bytes 110600 | tf_op jit(solution)/shard_map/ppermute | solution.py:432
  21.3 2.0 %collective-permute-start.2 = (bf16[328,128]{1,0:T(8,128)(2,1)S(1)}, bf16[328,128]{1,0:T(8,128)(2,1)S(1)}, u32[]{:S(2)}, u32[]{:S(2)}) collective-permute-start(bf16[328,128]{1,0:T(8,128)(2,1)S(1)} %get-tuple-element.85), channel_id=1, source_target_pairs={{0,1},{1,0},{2,3},{3,2},{4,5},{5,4},{6,7},{7,6},{8,9},{9,8},{10,11... | collective-permute-start | bytes 251912 | tf_op jit(solution)/shard_map/ppermute | solution.py:432
  23.3 1.5 %collective-permute-start.3 = (bf16[328,128]{1,0:T(8,128)(2,1)S(1)}, bf16[328,128]{1,0:T(8,128)(2,1)S(1)}, u32[]{:S(2)}, u32[]{:S(2)}) collective-permute-start(bf16[328,128]{1,0:T(8,128)(2,1)S(1)} %get-tuple-element.87), channel_id=1, source_target_pairs={{0,4},{1,5},{2,6},{3,7},{4,0},{5,1},{6,2},{7,3},{8,12},{9,13},{10,... | collective-permute-start | bytes 251912 | tf_op jit(solution)/shard_map/ppermute | solution.py:432
  24.9 1.2 %collective-permute-done.15 = bf16[144,128]{1,0:T(8,128)(2,1)S(1)} collective-permute-done((bf16[144,128]{1,0:T(8,128)(2,1)S(1)}, bf16[144,128]{1,0:T(8,128)(2,1)S(1)}, u32[]{:S(2)}, u32[]{:S(2)}) %collective-permute-start.15) | collective-permute-done | bytes 36896 | tf_op jit(solution)/shard_map/ppermute | solution.py:432
  26.1 1.8 %collective-permute-start.16 = (bf16[144,128]{1,0:T(8,128)(2,1)S(1)}, bf16[144,128]{1,0:T(8,128)(2,1)S(1)}, u32[]{:S(2)}, u32[]{:S(2)}) collective-permute-start(bf16[144,128]{1,0:T(8,128)(2,1)S(1)} %add_convert_fusion.3), channel_id=1, source_target_pairs={{0,8},{1,9},{2,10},{3,11},{4,12},{5,13},{6,14},{7,15},{8,0},{9,1},... | collective-permute-start | bytes 110600 | tf_op jit(solution)/shard_map/ppermute | solution.py:432
  27.9 2.6 %collective-permute-start.17 = (bf16[144,128]{1,0:T(8,128)(2,1)S(1)}, bf16[144,128]{1,0:T(8,128)(2,1)S(1)}, u32[]{:S(2)}, u32[]{:S(2)}) collective-permute-start(bf16[144,128]{1,0:T(8,128)(2,1)S(1)} %add_convert_fusion.3), channel_id=1, source_target_pairs={{0,16},{1,17},{2,18},{3,19},{4,20},{5,21},{6,22},{7,23},{8,24},{9,... | collective-permute-start | bytes 110600 | tf_op jit(solution)/shard_map/ppermute | solution.py:432
  30.6 1.3 %collective-permute-start.5 = (bf16[328,128]{1,0:T(8,128)(2,1)S(1)}, bf16[328,128]{1,0:T(8,128)(2,1)S(1)}, u32[]{:S(2)}, u32[]{:S(2)}) collective-permute-start(bf16[328,128]{1,0:T(8,128)(2,1)S(1)} %add_convert_fusion.1), channel_id=1, source_target_pairs={{0,8},{1,9},{2,10},{3,11},{4,12},{5,13},{6,14},{7,15},{8,0},{9,1},... | collective-permute-start | bytes 251912 | tf_op jit(solution)/shard_map/ppermute | solution.py:432
  31.9 3.1 %collective-permute-start.6 = (bf16[328,128]{1,0:T(8,128)(2,1)S(1)}, bf16[328,128]{1,0:T(8,128)(2,1)S(1)}, u32[]{:S(2)}, u32[]{:S(2)}) collective-permute-start(bf16[328,128]{1,0:T(8,128)(2,1)S(1)} %add_convert_fusion.1), channel_id=1, source_target_pairs={{0,16},{1,17},{2,18},{3,19},{4,20},{5,21},{6,22},{7,23},{8,24},{9,... | collective-permute-start | bytes 251912 | tf_op jit(solution)/shard_map/ppermute | solution.py:432
  35.1 1.2 %collective-permute-done.18 = bf16[144,128]{1,0:T(8,128)(2,1)S(1)} collective-permute-done((bf16[144,128]{1,0:T(8,128)(2,1)S(1)}, bf16[144,128]{1,0:T(8,128)(2,1)S(1)}, u32[]{:S(2)}, u32[]{:S(2)}) %collective-permute-start.18) | collective-permute-done | bytes 36896 | tf_op jit(solution)/shard_map/ppermute | solution.py:432
  37.1 1.5 %collective-permute-start.20 = (bf16[144,128]{1,0:T(8,128)(2,1)S(1)}, bf16[144,128]{1,0:T(8,128)(2,1)S(1)}, u32[]{:S(2)}, u32[]{:S(2)}) collective-permute-start(bf16[144,128]{1,0:T(8,128)(2,1)S(1)} %add_convert_fusion.2), channel_id=1, source_target_pairs={{0,4},{1,5},{2,6},{3,7},{4,0},{5,1},{6,2},{7,3},{8,12},{9,13},{10,... | collective-permute-start | bytes 110600 | tf_op jit(solution)/shard_map/ppermute | solution.py:432
  38.6 1.3 %collective-permute-start.21 = (bf16[144,128]{1,0:T(8,128)(2,1)S(1)}, bf16[144,128]{1,0:T(8,128)(2,1)S(1)}, u32[]{:S(2)}, u32[]{:S(2)}) collective-permute-start(bf16[144,128]{1,0:T(8,128)(2,1)S(1)} %add_convert_fusion.2), channel_id=1, source_target_pairs={{0,5},{1,4},{2,7},{3,6},{4,1},{5,0},{6,3},{7,2},{8,13},{9,12},{10,... | collective-permute-start | bytes 110600 | tf_op jit(solution)/shard_map/ppermute | solution.py:432
  39.9 1.4 %collective-permute-done.7 = bf16[328,128]{1,0:T(8,128)(2,1)S(1)} collective-permute-done((bf16[328,128]{1,0:T(8,128)(2,1)S(1)}, bf16[328,128]{1,0:T(8,128)(2,1)S(1)}, u32[]{:S(2)}, u32[]{:S(2)}) %collective-permute-start.7) | collective-permute-done | bytes 84000 | tf_op jit(solution)/shard_map/ppermute | solution.py:432
  42.1 1.5 %collective-permute-start.9 = (bf16[328,128]{1,0:T(8,128)(2,1)S(1)}, bf16[328,128]{1,0:T(8,128)(2,1)S(1)}, u32[]{:S(2)}, u32[]{:S(2)}) collective-permute-start(bf16[328,128]{1,0:T(8,128)(2,1)S(1)} %add_convert_fusion), channel_id=1, source_target_pairs={{0,4},{1,5},{2,6},{3,7},{4,0},{5,1},{6,2},{7,3},{8,12},{9,13},{10,... | collective-permute-start | bytes 251912 | tf_op jit(solution)/shard_map/ppermute | solution.py:432
  43.6 1.4 %collective-permute-start.10 = (bf16[328,128]{1,0:T(8,128)(2,1)S(1)}, bf16[328,128]{1,0:T(8,128)(2,1)S(1)}, u32[]{:S(2)}, u32[]{:S(2)}) collective-permute-start(bf16[328,128]{1,0:T(8,128)(2,1)S(1)} %add_convert_fusion), channel_id=1, source_target_pairs={{0,5},{1,4},{2,7},{3,6},{4,1},{5,0},{6,3},{7,2},{8,13},{9,12},{10,... | collective-permute-start | bytes 251912 | tf_op jit(solution)/shard_map/ppermute | solution.py:432
  46.5 2.4 %collective-permute-done.10 = bf16[328,128]{1,0:T(8,128)(2,1)S(1)} collective-permute-done((bf16[328,128]{1,0:T(8,128)(2,1)S(1)}, bf16[328,128]{1,0:T(8,128)(2,1)S(1)}, u32[]{:S(2)}, u32[]{:S(2)}) %collective-permute-start.10) | collective-permute-done | bytes 84000 | tf_op jit(solution)/shard_map/ppermute | solution.py:432
  49.7 1.2 %collective-permute-done.22.other_ref = bf16[576,128]{1,0:T(8,128)(2,1)S(1)} collective-permute-done((bf16[576,128]{1,0:T(8,128)(2,1)S(1)}, bf16[576,128]{1,0:T(8,128)(2,1)S(1)}, u32[]{:S(2)}, u32[]{:S(2)}) %collective-permute-start.22) | collective-permute-done | bytes 147488 | tf_op jit(solution)/shard_map/ppermute | solution.py:432
  51.0 1.4 %shard_map.133 = (f32[64,256]{1,0:T(8,128)}, f32[1024,128]{1,0:T(8,128)}) custom-call(s32[2]{0:T(128)S(1)} %pad_add_fusion.where_ref, bf16[576,128]{1,0:T(8,128)(2,1)S(1)} %pad_maximum_fusion.3.mine_ref, bf16[576,128]{1,0:T(8,128)(2,1)S(1)} %collective-permute-done.22.other_ref), custom_call_target="tpu_custom_call" | custom-call | tf_op jit(solution)/shard_map/pallas_call | solution.py:421
  52.4 1.7 %shard_map.132 = (f32[5,256,256]{2,1,0:T(8,128)}, f32[5,256]{1,0:T(8,128)}) custom-call(s32[2]{0:T(128)S(1)} %pad_add_fusion.where_ref, bf16[1312,128]{1,0:T(8,128)(2,1)S(1)} %pad_maximum_fusion.1.mine_ref, bf16[1312,128]{1,0:T(8,128)(2,1)S(1)} %collective-permute-done.11.other_ref), custom_call_target="tpu_custom_call" | custom-call | tf_op jit(solution)/shard_map/pallas_call | solution.py:421
  (43 shorter events, 6.8 us)
Async XLA Ops:
  4.8 5.1 %collective-permute-start = (bf16[192,128]{1,0:T(8,128)(2,1)S(1)}, bf16[192,128]{1,0:T(8,128)(2,1)S(1)}, u32[]{:S(2)}, u32[]{:S(2)}) collective-permute-start(bf16[192,128]{1,0:T(8,128)(2,1)S(1)} %bitcast.35), channel_id=1, source_target_pairs={{0,1},{1,0},{2,3},{3,2},{4,5},{5,4},{6,7},{7,6},{8,9},{9,8},{10,11... | collective-permute-start | bytes 147464 | tf_op jit(solution)/shard_map/ppermute | solution.py:502
  12.4 4.2 %collective-permute-start.12 = (bf16[576,128]{1,0:T(8,128)(2,1)S(1)}, bf16[576,128]{1,0:T(8,128)(2,1)}, u32[]{:S(2)}, u32[]{:S(2)}) collective-permute-start(bf16[576,128]{1,0:T(8,128)(2,1)S(1)} %get-tuple-element.82), channel_id=1, source_target_pairs={{0,2},{1,3},{2,0},{3,1},{4,6},{5,7},{6,4},{7,5},{8,10},{9,11},{10,... | collective-permute-start | bytes 442376 | tf_op jit(solution)/shard_map/ppermute | solution.py:432
  16.2 5.0 %collective-permute-start.1 = (bf16[1312,128]{1,0:T(8,128)(2,1)S(1)}, bf16[1312,128]{1,0:T(8,128)(2,1)S(1)}, u32[]{:S(2)}, u32[]{:S(2)}) collective-permute-start(bf16[1312,128]{1,0:T(8,128)(2,1)S(1)} %get-tuple-element.78), channel_id=1, source_target_pairs={{0,2},{1,3},{2,0},{3,1},{4,6},{5,7},{6,4},{7,5},{8,10},{9,11},{10,... | collective-permute-start | bytes 1007624 | tf_op jit(solution)/shard_map/ppermute | solution.py:432
  17.5 7.3 %collective-permute-start.13 = (bf16[144,128]{1,0:T(8,128)(2,1)S(1)}, bf16[144,128]{1,0:T(8,128)(2,1)S(1)}, u32[]{:S(2)}, u32[]{:S(2)}) collective-permute-start(bf16[144,128]{1,0:T(8,128)(2,1)S(1)} %get-tuple-element.92), channel_id=1, source_target_pairs={{0,1},{1,0},{2,3},{3,2},{4,5},{5,4},{6,7},{7,6},{8,9},{9,8},{10,11... | collective-permute-start | bytes 110600 | tf_op jit(solution)/shard_map/ppermute | solution.py:432
  19.6 5.3 %collective-permute-start.14 = (bf16[144,128]{1,0:T(8,128)(2,1)S(1)}, bf16[144,128]{1,0:T(8,128)(2,1)S(1)}, u32[]{:S(2)}, u32[]{:S(2)}) collective-permute-start(bf16[144,128]{1,0:T(8,128)(2,1)S(1)} %get-tuple-element.94), channel_id=1, source_target_pairs={{0,4},{1,5},{2,6},{3,7},{4,0},{5,1},{6,2},{7,3},{8,12},{9,13},{10,... | collective-permute-start | bytes 110600 | tf_op jit(solution)/shard_map/ppermute | solution.py:432
  21.1 5.0 %collective-permute-start.15 = (bf16[144,128]{1,0:T(8,128)(2,1)S(1)}, bf16[144,128]{1,0:T(8,128)(2,1)S(1)}, u32[]{:S(2)}, u32[]{:S(2)}) collective-permute-start(bf16[144,128]{1,0:T(8,128)(2,1)S(1)} %get-tuple-element.93), channel_id=1, source_target_pairs={{0,5},{1,4},{2,7},{3,6},{4,1},{5,0},{6,3},{7,2},{8,13},{9,12},{10,... | collective-permute-start | bytes 110600 | tf_op jit(solution)/shard_map/ppermute | solution.py:432
  21.3 9.1 %collective-permute-start.2 = (bf16[328,128]{1,0:T(8,128)(2,1)S(1)}, bf16[328,128]{1,0:T(8,128)(2,1)S(1)}, u32[]{:S(2)}, u32[]{:S(2)}) collective-permute-start(bf16[328,128]{1,0:T(8,128)(2,1)S(1)} %get-tuple-element.85), channel_id=1, source_target_pairs={{0,1},{1,0},{2,3},{3,2},{4,5},{5,4},{6,7},{7,6},{8,9},{9,8},{10,11... | collective-permute-start | bytes 251912 | tf_op jit(solution)/shard_map/ppermute | solution.py:432
  23.3 7.2 %collective-permute-start.3 = (bf16[328,128]{1,0:T(8,128)(2,1)S(1)}, bf16[328,128]{1,0:T(8,128)(2,1)S(1)}, u32[]{:S(2)}, u32[]{:S(2)}) collective-permute-start(bf16[328,128]{1,0:T(8,128)(2,1)S(1)} %get-tuple-element.87), channel_id=1, source_target_pairs={{0,4},{1,5},{2,6},{3,7},{4,0},{5,1},{6,2},{7,3},{8,12},{9,13},{10,... | collective-permute-start | bytes 251912 | tf_op jit(solution)/shard_map/ppermute | solution.py:432
  24.8 5.7 %collective-permute-start.4 = (bf16[328,128]{1,0:T(8,128)(2,1)S(1)}, bf16[328,128]{1,0:T(8,128)(2,1)S(1)}, u32[]{:S(2)}, u32[]{:S(2)}) collective-permute-start(bf16[328,128]{1,0:T(8,128)(2,1)S(1)} %get-tuple-element.86), channel_id=1, source_target_pairs={{0,5},{1,4},{2,7},{3,6},{4,1},{5,0},{6,3},{7,2},{8,13},{9,12},{10,... | collective-permute-start | bytes 251912 | tf_op jit(solution)/shard_map/ppermute | solution.py:432
  26.1 8.9 %collective-permute-start.16 = (bf16[144,128]{1,0:T(8,128)(2,1)S(1)}, bf16[144,128]{1,0:T(8,128)(2,1)S(1)}, u32[]{:S(2)}, u32[]{:S(2)}) collective-permute-start(bf16[144,128]{1,0:T(8,128)(2,1)S(1)} %add_convert_fusion.3), channel_id=1, source_target_pairs={{0,8},{1,9},{2,10},{3,11},{4,12},{5,13},{6,14},{7,15},{8,0},{9,1},... | collective-permute-start | bytes 110600 | tf_op jit(solution)/shard_map/ppermute | solution.py:432
  27.9 7.2 %collective-permute-start.17 = (bf16[144,128]{1,0:T(8,128)(2,1)S(1)}, bf16[144,128]{1,0:T(8,128)(2,1)S(1)}, u32[]{:S(2)}, u32[]{:S(2)}) collective-permute-start(bf16[144,128]{1,0:T(8,128)(2,1)S(1)} %add_convert_fusion.3), channel_id=1, source_target_pairs={{0,16},{1,17},{2,18},{3,19},{4,20},{5,21},{6,22},{7,23},{8,24},{9,... | collective-permute-start | bytes 110600 | tf_op jit(solution)/shard_map/ppermute | solution.py:432
  30.4 5.9 %collective-permute-start.18 = (bf16[144,128]{1,0:T(8,128)(2,1)S(1)}, bf16[144,128]{1,0:T(8,128)(2,1)S(1)}, u32[]{:S(2)}, u32[]{:S(2)}) collective-permute-start(bf16[144,128]{1,0:T(8,128)(2,1)S(1)} %add_convert_fusion.3), channel_id=1, source_target_pairs={{0,24},{1,25},{2,26},{3,27},{4,28},{5,29},{6,30},{7,31},{8,16},{9,... | collective-permute-start | bytes 110600 | tf_op jit(solution)/shard_map/ppermute | solution.py:432
  30.6 8.0 %collective-permute-start.5 = (bf16[328,128]{1,0:T(8,128)(2,1)S(1)}, bf16[328,128]{1,0:T(8,128)(2,1)S(1)}, u32[]{:S(2)}, u32[]{:S(2)}) collective-permute-start(bf16[328,128]{1,0:T(8,128)(2,1)S(1)} %add_convert_fusion.1), channel_id=1, source_target_pairs={{0,8},{1,9},{2,10},{3,11},{4,12},{5,13},{6,14},{7,15},{8,0},{9,1},... | collective-permute-start | bytes 251912 | tf_op jit(solution)/shard_map/ppermute | solution.py:432
  31.9 8.0 %collective-permute-start.6 = (bf16[328,128]{1,0:T(8,128)(2,1)S(1)}, bf16[328,128]{1,0:T(8,128)(2,1)S(1)}, u32[]{:S(2)}, u32[]{:S(2)}) collective-permute-start(bf16[328,128]{1,0:T(8,128)(2,1)S(1)} %add_convert_fusion.1), channel_id=1, source_target_pairs={{0,16},{1,17},{2,18},{3,19},{4,20},{5,21},{6,22},{7,23},{8,24},{9,... | collective-permute-start | bytes 251912 | tf_op jit(solution)/shard_map/ppermute | solution.py:432
  35.0 6.4 %collective-permute-start.7 = (bf16[328,128]{1,0:T(8,128)(2,1)S(1)}, bf16[328,128]{1,0:T(8,128)(2,1)S(1)}, u32[]{:S(2)}, u32[]{:S(2)}) collective-permute-start(bf16[328,128]{1,0:T(8,128)(2,1)S(1)} %add_convert_fusion.1), channel_id=1, source_target_pairs={{0,24},{1,25},{2,26},{3,27},{4,28},{5,29},{6,30},{7,31},{8,16},{9,... | collective-permute-start | bytes 251912 | tf_op jit(solution)/shard_map/ppermute | solution.py:432
  36.3 7.2 %collective-permute-start.19 = (bf16[144,128]{1,0:T(8,128)(2,1)S(1)}, bf16[144,128]{1,0:T(8,128)(2,1)S(1)}, u32[]{:S(2)}, u32[]{:S(2)}) collective-permute-start(bf16[144,128]{1,0:T(8,128)(2,1)S(1)} %add_convert_fusion.2), channel_id=1, source_target_pairs={{0,1},{1,0},{2,3},{3,2},{4,5},{5,4},{6,7},{7,6},{8,9},{9,8},{10,11... | collective-permute-start | bytes 110600 | tf_op jit(solution)/shard_map/ppermute | solution.py:432
  37.1 7.9 %collective-permute-start.20 = (bf16[144,128]{1,0:T(8,128)(2,1)S(1)}, bf16[144,128]{1,0:T(8,128)(2,1)S(1)}, u32[]{:S(2)}, u32[]{:S(2)}) collective-permute-start(bf16[144,128]{1,0:T(8,128)(2,1)S(1)} %add_convert_fusion.2), channel_id=1, source_target_pairs={{0,4},{1,5},{2,6},{3,7},{4,0},{5,1},{6,2},{7,3},{8,12},{9,13},{10,... | collective-permute-start | bytes 110600 | tf_op jit(solution)/shard_map/ppermute | solution.py:432
  38.6 6.4 %collective-permute-start.21 = (bf16[144,128]{1,0:T(8,128)(2,1)S(1)}, bf16[144,128]{1,0:T(8,128)(2,1)S(1)}, u32[]{:S(2)}, u32[]{:S(2)}) collective-permute-start(bf16[144,128]{1,0:T(8,128)(2,1)S(1)} %add_convert_fusion.2), channel_id=1, source_target_pairs={{0,5},{1,4},{2,7},{3,6},{4,1},{5,0},{6,3},{7,2},{8,13},{9,12},{10,... | collective-permute-start | bytes 110600 | tf_op jit(solution)/shard_map/ppermute | solution.py:432
  41.4 4.5 %collective-permute-start.8 = (bf16[328,128]{1,0:T(8,128)(2,1)S(1)}, bf16[328,128]{1,0:T(8,128)(2,1)S(1)}, u32[]{:S(2)}, u32[]{:S(2)}) collective-permute-start(bf16[328,128]{1,0:T(8,128)(2,1)S(1)} %add_convert_fusion), channel_id=1, source_target_pairs={{0,1},{1,0},{2,3},{3,2},{4,5},{5,4},{6,7},{7,6},{8,9},{9,8},{10,11... | collective-permute-start | bytes 251912 | tf_op jit(solution)/shard_map/ppermute | solution.py:432
  42.1 4.5 %collective-permute-start.9 = (bf16[328,128]{1,0:T(8,128)(2,1)S(1)}, bf16[328,128]{1,0:T(8,128)(2,1)S(1)}, u32[]{:S(2)}, u32[]{:S(2)}) collective-permute-start(bf16[328,128]{1,0:T(8,128)(2,1)S(1)} %add_convert_fusion), channel_id=1, source_target_pairs={{0,4},{1,5},{2,6},{3,7},{4,0},{5,1},{6,2},{7,3},{8,12},{9,13},{10,... | collective-permute-start | bytes 251912 | tf_op jit(solution)/shard_map/ppermute | solution.py:432
  43.6 5.4 %collective-permute-start.10 = (bf16[328,128]{1,0:T(8,128)(2,1)S(1)}, bf16[328,128]{1,0:T(8,128)(2,1)S(1)}, u32[]{:S(2)}, u32[]{:S(2)}) collective-permute-start(bf16[328,128]{1,0:T(8,128)(2,1)S(1)} %add_convert_fusion), channel_id=1, source_target_pairs={{0,5},{1,4},{2,7},{3,6},{4,1},{5,0},{6,3},{7,2},{8,13},{9,12},{10,... | collective-permute-start | bytes 251912 | tf_op jit(solution)/shard_map/ppermute | solution.py:432
  49.1 3.3 %collective-permute-start.11 = (bf16[1312,128]{1,0:T(8,128)(2,1)S(1)}, bf16[1312,128]{1,0:T(8,128)(2,1)S(1)}, u32[]{:S(2)}, u32[]{:S(2)}) collective-permute-start(bf16[1312,128]{1,0:T(8,128)(2,1)S(1)} %pad_maximum_fusion.1.mine_ref), channel_id=1, source_target_pairs={{0,2},{1,3},{2,0},{3,1},{4,6},{5,7},{6,4},{7,5},{8,10},{9,11},{10,... | collective-permute-start | bytes 1007624 | tf_op jit(solution)/shard_map/ppermute | solution.py:432
  49.2 1.8 %collective-permute-start.22 = (bf16[576,128]{1,0:T(8,128)(2,1)S(1)}, bf16[576,128]{1,0:T(8,128)(2,1)S(1)}, u32[]{:S(2)}, u32[]{:S(2)}) collective-permute-start(bf16[576,128]{1,0:T(8,128)(2,1)S(1)} %pad_maximum_fusion.3.mine_ref), channel_id=1, source_target_pairs={{0,2},{1,3},{2,0},{3,1},{4,6},{5,7},{6,4},{7,5},{8,10},{9,11},{10,... | collective-permute-start | bytes 442376 | tf_op jit(solution)/shard_map/ppermute | solution.py:432
